TPU v7x, 128 devices: a whole 4x4x4 slice. The times are simulated.
128 devices in a mesh: row: 8 (over x, core), col: 16 (over y, z).
Axes of the slice: x: 4, y: 4, z: 4, core: 2. Of those that a mesh axis runs over, the one named last changes fastest.
Arguments:
- centroid: float32 [3, 131072], P(None, ('row', 'col')), may hold values from -6 to 6
- normals: float32 [3, 131072], P(None, ('row', 'col')), may hold values from -3 to 3
- tangent: float32 [3, 131072], P(None, ('row', 'col')), may hold values from -3 to 3
- element_area: float32 [131072], P(('row', 'col')), may hold values from 0.01 to 0.04
- forward_field: float32 [2, 131072], P(None, ('row', 'col')), may hold values from -6 to 6
- adjoint_field: float32 [2, 131072], P(None, ('row', 'col')), may hold values from -6 to 6
- corners: int32 [3, 131072], P(None, ('row', 'col')), may hold values from 0 to 65535, as said below
- slot_map: int32 [65536], replicated, may hold values from 0 to 65535, as said below
- quad_order: int32 [128, 8, 16, 8], P('row', None, 'col'), may hold values from 0 to 2
- morph_modes: float32 [300, 6, 65536], P(None, None, ('row', 'col')), may hold values from -0.3 to 0.3
Outputs:
- vertex_partial: float32 [6, 65536], P(None, ('row', 'col'))
- mode_gradient: float32 [300], replicated
Inputs may be any that keep to these rules, and one draw needn't show every extreme that they name: slot_map is a permutation of 0 to 65535. `corners`: for each shard of elements (elements b * 1024 to (b + 1) * 1024 - 1), its 3072 corner references map through slot_map onto the slots of any one patch at most 24 times, and exactly 24 times for some patch.
All inputs are finite; a program needn't handle non-finite values.
Results may differ from a plain program's by a relative error of at most 0.0003.
Values sent between devices are 32-bit elements; how exact they have to be, the bound alone decides.
A program may use at most 128 MiB of HBM per device.

v0:
```python
import math

import jax
import jax.numpy as jnp
from jax import lax
from jax.sharding import PartitionSpec as P

SLAB_DEV = 8


wavenumber = 4.0
quad_offsets = (-0.6, 0.0, 0.6)
quad_table = ((0.0, 1.0, 0.0), (0.5, 0.0, 0.5), (1.0 / 3.0, 1.0 / 3.0, 1.0 / 3.0))


def point_weights(pair_flags, point_index):
    weight_sum = jnp.zeros(pair_flags.shape, jnp.float32)
    for flag_level in range(3):
        chosen = jnp.where(pair_flags == flag_level, quad_table[flag_level][point_index], 0.0)
        weight_sum = weight_sum + chosen.astype(jnp.float32)
    return weight_sum


def pair_terms(
    row_point, row_adjoint, col_point, col_normal, col_tangent, col_area, col_forward, pair_flags
):
    row_count = row_point.shape[1]
    col_count = col_point.shape[1]
    row_total = jnp.zeros((3, row_count), jnp.float32)
    col_total = jnp.zeros((3, col_count), jnp.float32)
    normal_total = jnp.zeros((3, col_count), jnp.float32)
    real_coupling = (
        row_adjoint[0][:, None] * col_forward[0][None, :]
        + row_adjoint[1][:, None] * col_forward[1][None, :]
    )
    imag_coupling = (
        row_adjoint[0][:, None] * col_forward[1][None, :]
        - row_adjoint[1][:, None] * col_forward[0][None, :]
    )
    spread = jnp.sqrt(col_area)
    for point_index in range(3):
        weight = point_weights(pair_flags, point_index) * col_area[None, :]
        source = col_point + quad_offsets[point_index] * spread[None, :] * col_tangent
        offset = row_point[:, :, None] - source[:, None, :]
        radius_sq = jnp.sum(offset * offset, axis=0) + col_area[None, :]
        radius = jnp.sqrt(radius_sq)
        phase_arg = wavenumber * radius
        cosine = jnp.cos(phase_arg)
        sine_part = jnp.sin(phase_arg)
        scale_three = 1.0 / (4.0 * math.pi * radius * radius_sq)
        scale_five = scale_three / radius_sq
        first_real = (-cosine - phase_arg * sine_part) * scale_three
        first_imag = (-sine_part + phase_arg * cosine) * scale_three
        poly_real = 3.0 - phase_arg * phase_arg
        poly_imag = -3.0 * phase_arg
        second_real = (cosine * poly_real - sine_part * poly_imag) * scale_five
        second_imag = (sine_part * poly_real + cosine * poly_imag) * scale_five
        along_normal = jnp.sum(offset * col_normal[:, None, :], axis=0)
        combo_real = -first_imag / wavenumber - second_real * along_normal
        combo_imag = first_real / wavenumber - second_imag * along_normal
        coeff_first = (real_coupling * first_real - imag_coupling * first_imag) * weight
        coeff_second = (real_coupling * combo_real - imag_coupling * combo_imag) * weight
        position = coeff_second[None] * offset - coeff_first[None] * col_normal[:, None, :]
        row_total = row_total + jnp.sum(position, axis=2)
        col_total = col_total - jnp.sum(position, axis=1)
        normal_total = normal_total - jnp.sum(coeff_first[None] * offset, axis=1)
    return (row_total, col_total, normal_total)


def body(
    centroid,
    normals,
    tangent,
    element_area,
    forward_field,
    adjoint_field,
    corners,
    slot_map,
    quad_order,
    morph_modes,
):
    local_count = centroid.shape[1]
    col_pack = jnp.concatenate(
        [centroid, normals, tangent, element_area[None, :], forward_field], axis=0
    )
    col_blocks = lax.all_gather(col_pack[None], "row", axis=0, tiled=True)
    slab_pack = jnp.concatenate([centroid[:, :SLAB_DEV], adjoint_field[:, :SLAB_DEV]], axis=0)
    slab_gathered = lax.all_gather(slab_pack, "col", axis=1, tiled=True)
    row_point = slab_gathered[0:3]
    row_adjoint = slab_gathered[3:5]
    block_flags = jnp.transpose(quad_order[:, :, 0, :], (1, 0, 2))
    tile_width = local_count // block_flags.shape[2]

    def visit_block(row_carry, inputs):
        column_block, tile_flags = inputs
        pair_flags = jnp.repeat(jnp.repeat(tile_flags, SLAB_DEV, axis=0), tile_width, axis=1)
        row_total, col_total, normal_total = pair_terms(
            row_point,
            row_adjoint,
            column_block[0:3],
            column_block[3:6],
            column_block[6:9],
            column_block[9],
            column_block[10:12],
            pair_flags,
        )
        return (row_carry + row_total, jnp.concatenate([col_total, normal_total], axis=0))

    row_sum, col_parts = lax.scan(
        visit_block, jnp.zeros(row_point.shape, jnp.float32), (col_blocks, block_flags)
    )
    own_columns = lax.psum_scatter(col_parts, "row", scatter_dimension=0, tiled=True)[0]
    own_rows = lax.psum_scatter(row_sum, "col", scatter_dimension=1, tiled=True)
    row_whole = jnp.pad(own_rows, ((0, 3), (0, local_count - SLAB_DEV)))
    element_part = own_columns + row_whole
    slot_ids = slot_map[corners].reshape(-1)
    values = jnp.concatenate([(element_part / 3.0).T] * 3, axis=0)
    dense_vertex = jax.ops.segment_sum(values, slot_ids, num_segments=slot_map.shape[0]).T
    vertex_partial = lax.psum_scatter(dense_vertex, ("row", "col"), scatter_dimension=1, tiled=True)
    projected = jnp.dot(
        morph_modes.reshape(morph_modes.shape[0], -1),
        vertex_partial.reshape(-1),
        precision=lax.Precision.HIGHEST,
    )
    mode_gradient = lax.psum(projected, ("row", "col"))
    return (vertex_partial, mode_gradient)


def solution(mesh):
    return jax.shard_map(
        body,
        mesh=mesh,
        in_specs=(
            P(None, ("row", "col")),
            P(None, ("row", "col")),
            P(None, ("row", "col")),
            P(("row", "col")),
            P(None, ("row", "col")),
            P(None, ("row", "col")),
            P(None, ("row", "col")),
            P(),
            P("row", None, "col", None),
            P(None, None, ("row", "col")),
        ),
        out_specs=(P(None, ("row", "col")), P()),
        check_vma=False,
    )
```

profile of v0, /device:TPU:1, one launch (start us, length us, event | category | flops | bytes accessed | tf_op | source)
XLA Modules:
  0.0 1022.6 jit_solution(6862774086173735548)
XLA Ops:
  7.2 0.7 slice.87
  8.9 20.5 %all_gather.6 = f32[5,128]{0,1:T(8,128)S(1)} all-gather(f32[5,8]{0,1:T(8,128)S(1)} %pad_maximum_fusion.1), channel_id=1, replica_groups=mesh['row'=8,'col'=16] {'col'}, dimensions={1}, use_global_device_ids=true | all-gather | bytes 2720 | tf_op jit(solution)/shard_map/all_gather | solution.py:88
  29.6 2.4 concatenate.17
  32.0 19.5 %all-gather.1 = f32[8,12,1024]{2,1,0:T(8,128)S(1)} all-gather(f32[1,12,1024]{2,1,0:T(8,128)S(1)} %bitcast.121), channel_id=2, replica_groups=mesh['row'=8,'col'=16] {'row'}, dimensions={0}, use_global_device_ids=true | all-gather | bytes 442368 | tf_op jit(solution)/shard_map/all_gather | solution.py:86
  51.5 108.5 %while.16 = (s32[]{:T(128)}, f32[3,128]{1,0:T(4,128)S(1)}, f32[8,6,1024]{2,1,0:T(8,128)S(1)}, f32[2,128]{1,0:T(2,128)S(1)}, f32[8,12,1024]{2,1,0:T(8,128)S(1)}, ...) while((s32[]{:T(128)}, f32[3,128]{1,0:T(4,128)S(1)}, ...), condition=%wide.region_16.17_spmd.clone, body=%wide.region_0.16_spmd.clone.sunk | while | flops 32666120 | bytes 15759359 | solution.py:109
  51.5 0.7 fusion.37
  53.9 3.0 subtract_multiply_fusion.23
  56.9 1.2 fusion.39
  58.1 5.7 subtract_multiply_fusion.24
  63.8 1.2 fusion.40
  65.0 0.7 fusion.37
  67.5 3.0 subtract_multiply_fusion.23
  70.4 1.2 fusion.39
  71.6 5.7 subtract_multiply_fusion.24
  77.3 1.2 fusion.40
  81.0 3.0 subtract_multiply_fusion.23
  84.0 1.2 fusion.39
  85.2 5.7 subtract_multiply_fusion.24
  90.9 1.2 fusion.40
  94.6 3.0 subtract_multiply_fusion.23
  97.6 1.2 fusion.39
  98.8 5.7 subtract_multiply_fusion.24
  104.5 1.2 fusion.40
  108.2 3.0 subtract_multiply_fusion.23
  111.1 1.2 fusion.39
  112.4 5.7 subtract_multiply_fusion.24
  118.0 1.2 fusion.40
  121.7 3.0 subtract_multiply_fusion.23
  124.7 1.2 fusion.39
  125.9 5.7 subtract_multiply_fusion.24
  131.6 1.2 fusion.40
  135.3 3.0 subtract_multiply_fusion.23
  138.3 1.2 fusion.39
  139.5 5.7 subtract_multiply_fusion.24
  145.2 1.2 fusion.40
  148.9 3.0 subtract_multiply_fusion.23
  151.8 1.2 fusion.39
  153.1 5.7 subtract_multiply_fusion.24
  158.7 1.2 fusion.40
  162.1 17.4 %gather_fusion = s32[3072]{0:T(1024)S(1)} fusion(s32[65536]{0:T(1024)S(1)} %copy-done, s32[3072]{0:T(1024)S(1)} %broadcast_clamp_fusion), kind=kCustom, calls=%fused_computation | custom fusion | bytes 36864 | tf_op jit(solution)/shard_map/gather | solution.py:116
  179.5 31.2 %all-reduce.1 = f32[3,128]{1,0:T(4,128)S(1)} all-reduce(f32[3,128]{1,0:T(4,128)S(1)} %get-tuple-element.114), channel_id=4, replica_groups=mesh['row'=8,'col'=16] {'col'}, use_global_device_ids=true, to_apply=%region_18.19.clone | all-reduce | flops 384 | bytes 3072
  210.8 0.8 fusion.27
  212.1 30.1 %scatter_custom_fusion = f32[65536,6]{1,0:T(8,128)} fusion(s32[3072]{0:T(1024)S(1)} %gather_fusion, f32[3072,6]{1,0:T(8,128)S(1)} %copy.32, f32[]{:T(128)} %constant.121.clone.1), kind=kCustom, calls=%fused_computation.86 | custom fusion | flops 18432 | bytes 1572868 | tf_op jit(solution)/shard_map/scatter-add | solution.py:118
  242.2 674.3 %reduce-scatter.6.cloned.1.call-done = f32[6,512]{0,1:T(8,128)} async-done(((f32[6,65536]{0,1:T(8,128)}), f32[6,512]{0,1:T(8,128)}) %reduce-scatter.6.cloned.1.call-update) | async-done | bytes 12304 | tf_op jit(solution)/shard_map/reduce_scatter | solution.py:119
  916.5 1.1 copy.34
  917.5 5.2 convolution_reduce_fusion
  922.7 92.4 %psum.7 = f32[300]{0:T(512)} all-reduce(f32[300]{0:T(512)S(1)} %convolution_reduce_fusion), channel_id=1, replica_groups=mesh['row'=8,'col'=16] {'row','col'}, use_global_device_ids=true, to_apply=%region_21.22 | all-reduce | flops 300 | bytes 2400 | tf_op jit(solution)/shard_map/psum | solution.py:125
  1015.1 0.7 copy.33
  (165 shorter events, 21.0 us)
Async XLA Ops:
  7.2 154.9 %copy-start = (s32[65536]{0:T(1024)S(1)}, s32[65536]{0:T(1024)}, u32[]{:S(2)}) copy-start(s32[65536]{0:T(1024)} %param.19) | copy-start | bytes 786436
  7.2 203.6 %reduce-scatter.4.cloned.1.call-start = ((), (), s32[]{:S(2)}) async-start(), calls=%async_computation.2 | async-start | bytes 294912 | tf_op jit(solution)/shard_map/reduce_scatter | solution.py:112
  51.4 109.3 %copy-start.3 = (s32[3,1024]{1,0:T(4,128)S(1)}, s32[3,1024]{1,0:T(4,128)}, u32[]{:S(2)}) copy-start(s32[3,1024]{1,0:T(4,128)} %param.18) | copy-start | bytes 36868
  51.4 109.4 %copy-start.4 = (u32[128]{0:T(128)S(1)}, u32[128]{0:T(128)}, u32[]{:S(2)}) copy-start(u32[128]{0:T(128)} %constant.130) | copy-start | bytes 1540
  160.0 0.7 copy-start.2
  160.7 755.7 %reduce-scatter.6.cloned.1.call-start = ((), (), s32[]{:S(2)}) async-start(), calls=%async_computation.3 | async-start | bytes 33816576 | tf_op jit(solution)/shard_map/reduce_scatter | solution.py:119
  917.5 97.6 %copy-start.1 = (f32[6,512]{0,1:T(8,128)S(1)}, f32[6,512]{0,1:T(8,128)}, u32[]{:S(2)}) copy-start(f32[6,512]{0,1:T(8,128)} %reduce-scatter.6.cloned.1.call-done) | copy-start | bytes 36868
Sparse Core Ops, SparseCore 0:
  160.8 26.3 reduce-scatter.3
  242.3 674.1 reduce-scatter.5
where the time goes:
time: 1020 us
  waiting for transfers between devices  674 us (66%)
  blocking collectives  164 us (16%)
  other arithmetic  134 us (13%)
  local copies, waits for them, and re-layouts  29.9 us (3%)
  between operations  14.8 us (1%)
    reduce_scatter x1, waiting for transfers between devices, body(): lax.psum_scatter(dense_vertex, ('row', 'col'), scatter_dimension=1, tiled...  674 us
    psum x1, blocking collectives, body(): mode_gradient = lax.psum(projected, ('row', 'col'))  92.4 us
    mul x16, other arithmetic, pair_terms(): (real_coupling * combo_real - imag_coupling * combo_imag) * weight  69 us
    unnamed x1, blocking collectives  31.2 us
    scatter-add x1, other arithmetic, body(): jax.ops.segment_sum(values, slot_ids, num_segments=slot_map.shape[0])  30.1 us
    all_gather x1, blocking collectives, body(): slab_gathered = lax.all_gather(slab_pack, 'col', axis=1, tiled=True)  20.5 us
  transfers between devices with their start and end apart: 2, of which 1 were waited for; matrix products, arithmetic and copies ran while one was open for 2% of the time, Pallas kernels for 0%

commit v1 on v0

v1 whole, which is shorter than its diff:
```python
import math, functools
import jax, jax.numpy as jnp
from jax import lax
from jax.experimental import pallas as pl
from jax.experimental.pallas import tpu as pltpu

F32 = jnp.float32
MAGIC = 12582912.0
INV_TURN = 1.0 / (2.0 * math.pi)
SIN_C = (4.442883014678955, -7.308245658874512, 3.6063544750213623, -0.8461129069328308, 0.10982698947191238)
COS_C = (1.4142135381698608, -6.978850841522217, 5.7394609451293945, -1.8835630416870117, 0.31069818139076233)


def horner(coeffs, z):
    total = z * coeffs[-1] + coeffs[-2]
    for value in coeffs[-3::-1]:
        total = total * z + value
    return total


def green(r2, cr, ci):
    inv = lax.rsqrt(r2)
    phi = r2 * inv
    turn = phi * INV_TURN
    frac = turn - ((turn + MAGIC) - MAGIC)
    z = frac * frac
    hs = frac * horner(SIN_C, z)
    hc = horner(COS_C, z)
    cosine = 1.0 - hs * hs
    sine = hs * hc
    er = cr * cosine - ci * sine
    ei = cr * sine + ci * cosine
    i2 = inv * inv
    i3 = i2 * inv
    g = er + phi * ei
    h = ei - phi * er
    k = g * (3.0 * i2) - er
    return g, h, k, i3


def tile_terms(kind, row, col, cr_scale, ci_scale):
    x, y, z, ar, ai = row
    dx, dy, dz = x - col["y"][0], y - col["y"][1], z - col["y"][2]
    d = (dx, dy, dz)
    nx, ny, nz = col["n"]
    mn = dx * nx + dy * ny + dz * nz
    sq = dx * dx + dy * dy + dz * dz
    cr = ar * cr_scale + ai * ci_scale
    ci = ar * ci_scale - ai * cr_scale
    out = {}
    sa = sb = None
    if kind != 0:
        ex, ey, ez = col["t2"]
        e = dx * ex + dy * ey + dz * ez
        b = sq + col["at"]
        pts = []
        for sign in (-1, 1):
            if sign > 0:
                r2, m = b - e, mn - col["tn"]
            else:
                r2, m = b + e, mn + col["tn"]
            g, h, k, i3 = green(r2, cr, ci)
            pts.append((i3 * g, i3 * (h - m * k)))
        (a0, b0), (a2, b2) = pts
        sa, sb, da, db = a0 + a2, b0 + b2, a2 - a0, b2 - b0
    if kind != 1:
        g, h, k, i3 = green(sq + col["a"], cr, ci)
        a1, b1 = i3 * g, i3 * (h - mn * k)
        sa, sb = (a1, b1) if sa is None else (sa + a1, sb + b1)
    bd = [sb * v for v in d]
    ad = [sa * v for v in d]
    an = [sa * v for v in (nx, ny, nz)]
    pos = [p + q for p, q in zip(bd, an)]
    if kind == 0:
        return pos, pos, ad, None
    ts = col["ts"]
    pos = [p - db * t for p, t in zip(pos, ts)]
    return pos, pos, ad, da


def pair_kernel(batches, groups, lists_ref, rows_ref, cen_ref, nor_ref, tan_ref, area_ref, fwd_ref, col_out, row_out, table, racc, ctab):
    tiles = lists_ref.shape[0]
    rt = jnp.transpose(rows_ref[...])
    for g in range(groups):
        for q in range(5):
            v = jnp.broadcast_to(rt[q * 8:(q + 1) * 8, g:g + 1], (8, 128))
            table[g, q] = v * 4.0 if q < 3 else v
    table[groups] = jnp.concatenate([jnp.full((3, 8, 128), 1.0, F32), jnp.zeros((2, 8, 128), F32)], axis=0)
    racc[...] = jnp.zeros(racc.shape, F32)
    area = area_ref[...]
    spread = jnp.sqrt(area) * 2.4
    ysc = 4.0 * cen_ref[...]
    n16 = 16.0 * nor_ref[...]
    ts = spread * tan_ref[...]
    a16 = 16.0 * area
    at = a16 + jnp.sum(ts * ts, axis=0, keepdims=True)
    tn = jnp.sum(ts * n16, axis=0, keepdims=True)
    fw = fwd_ref[...] * (area * (1.0 / math.pi))
    rows = [ysc, n16, ts, 2.0 * ts, a16, at, tn, fw]
    pos = 0
    for r in rows:
        ctab[pos:pos + r.shape[0], :] = r
        pos += r.shape[0]

    def tile_body(t, _):
        lanes = pl.ds(pl.multiple_of(t * 128, 128), 128)

        def bc(i):
            return jnp.broadcast_to(ctab[i:i + 1, lanes], (8, 128))

        def getcol():
            return dict(y=[bc(0), bc(1), bc(2)], n=[bc(3), bc(4), bc(5)], ts=[bc(6), bc(7), bc(8)],
                        t2=[bc(9), bc(10), bc(11)], a=bc(12), at=bc(13), tn=bc(14))
        zero = jnp.zeros((8, 128), F32)
        n0, n1, n2 = lists_ref[t, 253], lists_ref[t, 254], lists_ref[t, 255]
        b0, b1, b2 = batches
        s0 = 0
        s1 = n0 * b0
        s2 = s1 + n1 * b1
        carry = (zero,) * 7

        def make(kind, size, start, weight):
            def body(it, acc):
                col = getcol()
                frs, fis = bc(15) * weight, bc(16) * weight
                acc = list(acc)
                ids, news = [], []
                for j in range(size):
                    g = lists_ref[t, start + it * size + j]
                    row = [table[g, q] for q in range(5)]
                    pos, cpos, ad, da = tile_terms(kind, row, col, frs, fis)
                    for q in range(3):
                        acc[q] = acc[q] + pos[q]
                        acc[3 + q] = acc[3 + q] + ad[q]
                    if da is not None:
                        acc[6] = acc[6] + da
                    ids.append(g)
                    news.append(pos)
                olds = [[racc[g, q] for q in range(3)] for g in ids]
                for g, old, new in zip(ids, olds, news):
                    for q in range(3):
                        racc[g, q] = old[q] + new[q]
                return tuple(acc)
            return body
        carry = lax.fori_loop(0, n0, make(0, b0, s0, 1.0), carry)
        carry = lax.fori_loop(0, n1, make(1, b1, s1, 0.5), carry)
        carry = lax.fori_loop(0, n2, make(2, b2, s2, 1.0 / 3.0), carry)
        sums = [jnp.sum(v, axis=0, keepdims=True) for v in carry]
        for q in range(3):
            col_out[q:q + 1, lanes] = -sums[q]
            tsr = ctab[6 + q:7 + q, lanes]
            col_out[3 + q:4 + q, lanes] = 4.0 * (sums[3 + q] - sums[6] * tsr)
        return 0

    lax.fori_loop(0, tiles, tile_body, 0)
    lane = lax.broadcasted_iota(jnp.int32, (8, 128), 1)
    outs = [jnp.zeros((8, 128), F32) for _ in range(3)]
    for g in range(groups):
        for q in range(3):
            s = jnp.sum(racc[g, q], axis=1, keepdims=True)
            outs[q] = jnp.where(lane == g, s, outs[q])
    full = jnp.concatenate(outs + [jnp.zeros((104, 128), F32)], axis=0)
    row_out[...] = jnp.transpose(full)


def pair_call(lists, rows, cen, nor, tan, area, fwd, batches=(8, 4, 4)):
    el = cen.shape[1]
    groups = rows.shape[0]
    vm = pl.BlockSpec(memory_space=pltpu.VMEM)
    return pl.pallas_call(
        functools.partial(pair_kernel, batches, groups),
        out_shape=(jax.ShapeDtypeStruct((6, el), F32), jax.ShapeDtypeStruct((128, 128), F32)),
        in_specs=[pl.BlockSpec(memory_space=pltpu.SMEM)] + [vm] * 6,
        out_specs=(vm, vm),
        scratch_shapes=[pltpu.VMEM((groups + 1, 5, 8, 128), F32), pltpu.VMEM((groups + 1, 3, 8, 128), F32),
                        pltpu.VMEM((24, el), F32)],
        name="pairs",
    )(lists, rows, cen, nor, tan, area, fwd)


def dot_nn(a, b):
    return lax.dot_general(a, b, (((1,), (0,)), ((), ())), preferred_element_type=F32)


def dot_nt(a, b):
    return lax.dot_general(a, b, (((1,), (1,)), ((), ())), preferred_element_type=F32)


def iota(shape, dim):
    return lax.broadcasted_iota(jnp.int32, shape, dim)


BF16 = jnp.bfloat16


def split3(v):
    hi = v.astype(BF16)
    rest = v - hi.astype(F32)
    mid = rest.astype(BF16)
    low = (rest - mid.astype(F32)).astype(BF16)
    return hi, mid, low


def ones_where(mask):
    return jnp.where(mask, 1.0, 0.0)


def make_lists(flags, batches):
    l0, l1 = iota((128, 128), 0), iota((128, 128), 1)
    same = (l0 & 7) == (l1 & 7)
    before = ones_where(same & (l0 < l1)).astype(BF16)
    same = ones_where(same).astype(BF16)
    lower = ones_where(iota((8, 8), 0) > iota((8, 8), 1)).astype(BF16)
    lane = iota((8, 128), 1)
    tile = iota((8, 128), 0)
    pick = ones_where(lane == tile).astype(BF16)
    pos = jnp.zeros((8, 128), F32)
    base = jnp.zeros((8, 128), F32)
    counts = []
    for kind in range(3):
        mask = ones_where(flags == float(kind))
        mb = mask.astype(BF16)
        rowtot = dot_nn(mb, same)
        inside = dot_nn(mb, before) + dot_nn(lower, rowtot.astype(BF16))
        total = jnp.sum(rowtot, axis=0, keepdims=True) + jnp.zeros((8, 128), F32)
        pos = pos + mask * (inside + base)
        nb = jnp.floor((total + float(batches[kind] - 1)) * (1.0 / batches[kind]))
        base = base + nb * float(batches[kind])
        counts.append(dot_nt(pick, nb.astype(BF16))[:, 0:1])
    posi = pos.astype(jnp.int32)
    slot = iota((256, 128), 0)
    out = jnp.zeros((8, 256), F32)
    for r in range(8):
        hit = ones_where(slot == posi[r:r + 1, :]).astype(BF16)
        value = jnp.where((lane & 7) == tile, ((lane >> 3) * 8 + (r - 128)).astype(F32), 0.0).astype(BF16)
        out = out + dot_nt(value, hit)
    out = out + 128.0
    wide = iota((8, 256), 1)
    for kind in range(3):
        out = jnp.where(wide == 253 + kind, counts[kind], out)
    return out.astype(jnp.int32)


def lookup_slots(table, corners):
    parts = jnp.concatenate([(table >> 8).astype(F32).astype(BF16), (table & 255).astype(F32).astype(BF16)], axis=1)
    width = 256
    lo_iota = iota((128, width), 0)
    hi_iota = iota((512, width), 0)
    rows = []
    for n in range(corners.shape[0]):
        pieces = []
        for cb in range(corners.shape[1] // width):
            v = corners[n:n + 1, cb * width:(cb + 1) * width]
            hit = lo_iota == (v & 127)
            rhs = jnp.concatenate([jnp.where(hit, 256.0, 0.0), jnp.where(hit, 1.0, 0.0)], axis=0).astype(BF16)
            sel = dot_nn(parts, rhs)
            pieces.append(jnp.sum(jnp.where(hi_iota == (v >> 7), sel, 0.0), axis=0, keepdims=True))
        rows.append(jnp.concatenate(pieces, axis=1))
    return jnp.concatenate(rows, axis=0).astype(jnp.int32)


def patch_ranks(patches):
    width = 256
    before = ones_where(iota((width, width), 0) < iota((width, width), 1)).astype(BF16)
    sub = iota((128, width), 0)
    carry = jnp.zeros((128, 1), F32)
    rows = []
    for n in range(patches.shape[0]):
        pieces = []
        for cb in range(patches.shape[1] // width):
            hit = ones_where(sub == patches[n:n + 1, cb * width:(cb + 1) * width])
            earlier = dot_nn(hit.astype(BF16), before) + carry
            pieces.append(jnp.sum(hit * earlier, axis=0, keepdims=True))
            carry = carry + jnp.sum(hit, axis=1, keepdims=True)
        rows.append(jnp.concatenate(pieces, axis=1))
    return jnp.concatenate(rows, axis=0)


def fill_buckets(values, slots, ranks):
    width = 256
    sub = iota((128, width), 0)
    rank_of_row = iota((192, width), 0) >> 3
    send = jnp.zeros((128, 192), F32)
    for n in range(slots.shape[0]):
        for cb in range(slots.shape[1] // width):
            cols = slice(cb * width, (cb + 1) * width)
            s = slots[n:n + 1, cols]
            hit = ones_where(sub == (s >> 9)).astype(BF16)
            eight = jnp.concatenate([values[:, cols], (s & 511).astype(F32), jnp.zeros((1, width), F32)], axis=0)
            mine = rank_of_row == ranks[n:n + 1, cols].astype(jnp.int32)
            for part in split3(eight):
                rhs = jnp.where(mine, jnp.concatenate([part.astype(F32)] * 24, axis=0), 0.0).astype(BF16)
                send = send + dot_nt(hit, rhs)
    return jnp.concatenate([send, jnp.zeros((128, 64), F32)], axis=1)


def add_up(recv):
    turned = jnp.transpose(recv)
    sub = iota((512, 128), 0).astype(F32)
    total = jnp.zeros((24, 512), F32)
    for pair in range(12):
        parts, hits = [], []
        for q in (2 * pair, 2 * pair + 1):
            eight = turned[q * 8:(q + 1) * 8, :]
            hits.append(ones_where(sub == eight[6:7, :]).astype(BF16))
            parts.append(jnp.concatenate([p.astype(F32) for p in split3(eight)], axis=0))
        lhs = jnp.concatenate(parts, axis=1).astype(BF16)
        total = total + dot_nt(lhs, jnp.concatenate(hits, axis=1))
    return total[0:8] + total[8:16] + total[16:24]


def lists_kernel(flags_ref, out_ref):
    out_ref[...] = make_lists(flags_ref[...], BATCHES)


def slots_kernel(table_ref, corners_ref, slots_ref, ranks_ref):
    slots = lookup_slots(table_ref[...], corners_ref[...])
    slots_ref[...] = slots
    ranks_ref[...] = patch_ranks(slots >> 9)


def bucket_kernel(values_ref, slots_ref, ranks_ref, out_ref):
    out_ref[...] = fill_buckets(values_ref[...], slots_ref[...], ranks_ref[...])


def project(modes_ref, vertex, acc_ref):
    count = modes_ref.shape[0]
    step = 10

    def visit(i, _):
        block = pl.ds(i * step, step)
        s = sum(modes_ref[block, :, k * 128:(k + 1) * 128] * vertex[None, 0:6, k * 128:(k + 1) * 128] for k in range(4))
        folded = jnp.sum(s, axis=1)
        acc_ref[block, :] = folded
        return 0
    lax.fori_loop(0, count // step, visit, 0, unroll=False)
    ones = jnp.ones((8, 128), BF16)
    return sum(dot_nt(ones, p) for p in split3(acc_ref[...]))


def vertex_kernel(recv_ref, modes_ref, vertex_ref, grad_ref, acc_ref):
    vertex = add_up(recv_ref[...])
    vertex_ref[...] = vertex[0:6]
    grad_ref[...] = project(modes_ref, vertex, acc_ref)[0:1]


VM = pl.BlockSpec(memory_space=pltpu.VMEM)
SLAB_DEV = 8
BATCHES = (8, 4, 4)


def simple(kernel, shapes, name, *args, scratch=()):
    return pl.pallas_call(kernel, out_shape=shapes, in_specs=[VM] * len(args),
                          out_specs=jax.tree.map(lambda _: VM, shapes), scratch_shapes=scratch, name=name)(*args)


S = jax.ShapeDtypeStruct
I32 = jnp.int32


def body(centroid, normals, tangent, element_area, forward_field, adjoint_field, corners, slot_map, quad_order, morph_modes):
    el = centroid.shape[1]
    slab = jnp.concatenate([centroid[:, :8], adjoint_field[:, :8]], axis=0).reshape(1, 40)
    slab = jnp.pad(slab, ((0, 0), (0, 88)))
    rows = lax.all_gather(slab, ("row", "col"), axis=0, tiled=True)
    rows = rows.reshape(8, 16, 128).transpose(1, 0, 2).reshape(128, 128)
    flags = quad_order[:, :, 0, :].transpose(1, 0, 2).reshape(8, 128).astype(F32)
    flags = lax.all_to_all(flags, "row", 0, 0, tiled=True)
    lists = simple(lists_kernel, S((8, 256), I32), "lists", flags)
    col_part, row_part = pair_call(lists, rows, centroid, normals, tangent, element_area[None, :], forward_field, BATCHES)
    row_part = row_part.reshape(16, 8, 128).transpose(1, 0, 2).reshape(128, 128)
    own = jnp.sum(lax.all_to_all(row_part, ("row", "col"), 0, 0, tiled=True), axis=0)[:24].reshape(3, 8)
    element_part = col_part + jnp.pad(own, ((0, 3), (0, el - 8)))
    slots, ranks = simple(slots_kernel, (S((3, el), I32), S((3, el), F32)), "slots", slot_map.reshape(512, 128), corners)
    send = simple(bucket_kernel, S((128, 256), F32), "buckets", element_part / 3.0, slots, ranks)
    recv = lax.all_to_all(send, ("row", "col"), 0, 0, tiled=True)
    vertex, grad = simple(vertex_kernel, (S((6, 512), F32), S((1, 300), F32)), "vertex", recv, morph_modes,
                          scratch=[pltpu.VMEM((300, 128), F32)])
    return vertex, lax.psum(grad[0], ("row", "col"))


def solution(mesh):
    from jax.sharding import PartitionSpec as P
    every = ("row", "col")
    return jax.shard_map(
        body, mesh=mesh,
        in_specs=(P(None, every), P(None, every), P(None, every), P(every), P(None, every), P(None, every), P(None, every),
                  P(), P("row", None, "col", None), P(None, None, every)),
        out_specs=(P(None, every), P()), check_vma=False)
```

time: 1020 us -> 197 us (0.19)
  waiting for transfers between devices: 674 us -> 9.71 us
  other arithmetic: 134 us -> 2.99 us
  blocking collectives: 164 us -> 111 us
  Pallas kernels: 0 us -> 41.7 us
  starting transfers between devices: 0.08 us -> 16.9 us
  local copies, waits for them, and re-layouts: 29.9 us -> 13.8 us
  between operations: 14.8 us -> 0.66 us
    reduce_scatter x2 -> x0, waiting for transfers between devices: 674 us -> none  [the longest x1 674 us: body(): lax.psum_scatter(dense_vertex, ('row', 'col'), scatter_dimension=1, tiled...]
    mul x24 -> x0, other arithmetic: 69.1 us -> none  [the longest x16 69 us: pair_terms(): (real_coupling * combo_real - imag_coupling * combo_imag) * weight]
    pallas_call x0 -> x5, Pallas kernels: none -> 41.7 us  [the longest x1 28.2 us: pair_call(): pl.pallas_call(functools.partial(pair_kernel, batches, groups), out_shape...]
    unnamed x1 -> x0, blocking collectives: 31.2 us -> none
    scatter-add x1 -> x0, other arithmetic: 30.1 us -> none  [body(): jax.ops.segment_sum(values, slot_ids, num_segments=slot_map.shape[0])]
    psum x1, blocking collectives: 92.4 us -> 63.6 us  [body(): return (vertex, lax.psum(grad[0], ('row', 'col')))]
    reduce_sum x24 -> x1, other arithmetic: 22.1 us -> 0.15 us  [body(): jnp.sum(lax.all_to_all(row_part, ('row', 'col'), 0, 0, tiled=True), axis=0)]
    gather x1 -> x0, local copies, waits for them, and re-layouts: 17.4 us -> none  [body(): slot_ids = slot_map[corners].reshape(-1)]
  transfers between devices with their start and end apart: 2 -> 3, of which waited for: 1 -> 2; matrix products, arithmetic and copies ran while one was open for 2% -> 4% of each run, Pallas kernels for 0% -> 2%
where the time goes in v1:
time: 197 us
  blocking collectives  111 us (56%)
  Pallas kernels  41.7 us (21%)
  starting transfers between devices  16.9 us (9%)
  local copies, waits for them, and re-layouts  13.8 us (7%)
  waiting for transfers between devices  9.71 us (5%)
  other arithmetic  2.99 us (2%)
    psum x1, blocking collectives, body(): return (vertex, lax.psum(grad[0], ('row', 'col')))  63.6 us
    all_gather x1, blocking collectives, body(): rows = lax.all_gather(slab, ('row', 'col'), axis=0, tiled=True)  47.2 us
    pallas_call x1, Pallas kernels, pair_call(): pl.pallas_call(functools.partial(pair_kernel, batches, groups), out_shape...  28.2 us
    pallas_call x4, Pallas kernels, simple(): pl.pallas_call(kernel, out_shape=shapes, in_specs=[VM] * len(args), out_s...  13.5 us
    unnamed x5, local copies, waits for them, and re-layouts  7.72 us
    all_to_all x1, starting transfers between devices, body(): lax.all_to_all(row_part, ('row', 'col'), 0, 0, tiled=True)  6.65 us
    all_to_all x1, waiting for transfers between devices, body(): lax.all_to_all(row_part, ('row', 'col'), 0, 0, tiled=True)  6.13 us
    all_to_all x1, starting transfers between devices, body(): flags = lax.all_to_all(flags, 'row', 0, 0, tiled=True)  5.79 us
  transfers between devices with their start and end apart: 3, of which 2 were waited for; matrix products, arithmetic and copies ran while one was open for 4% of the time, Pallas kernels for 2%

profile of v1, /device:TPU:1, one launch (start us, length us, event | category | flops | bytes accessed | tf_op | source)
XLA Modules:
  0.0 196.7 jit_solution(2486703106217944316)
XLA Ops:
  0.6 0.8 convert_bitcast_fusion
  1.4 0.1 copy.19
  1.5 0.7 convert_element_type.26
  2.2 5.8 %all-to-all-start = ((f32[8,1,128]{2,1,0:T(1,128)}), f32[8,1,128]{2,1,0:T(1,128)S(1)}, u32[]{:S(2)}, u32[]{:S(2)}) async-start(f32[8,1,128]{2,1,0:T(1,128)} %bitcast.2), calls=%async_computation | async-start | bytes 8192 | tf_op jit(solution)/shard_map/all_to_all | solution.py:368
  8.0 0.7 slice.18
  8.6 0.7 slice.17
  9.3 0.1 reshape.51
  9.4 47.2 %all-gather = f32[128,1,128]{2,1,0:T(1,128)S(1)} all-gather(f32[1,1,128]{2,1,0:T(1,128)S(1)} %pad_bitcast_fusion), channel_id=1, replica_groups=mesh['row'=8,'col'=16] {'row','col'}, dimensions={0}, use_global_device_ids=true | all-gather | bytes 66048 | tf_op jit(solution)/shard_map/all_gather | solution.py:365
  56.6 0.6 copy.30
  57.3 0.0 all-to-all-done
  57.3 0.0 copy-start
  57.3 0.6 copy-done
  57.9 2.1 %lists.1.lists_ref = s32[8,256]{1,0:T(8,128)} custom-call(f32[8,128]{1,0:T(8,128)} %bitcast.33), custom_call_target="tpu_custom_call" | custom-call | tf_op jit(solution)/shard_map/lists/pallas_call | solution.py:353
  60.0 28.2 %pairs.1 = (f32[6,1024]{1,0:T(8,128)}, f32[128,128]{1,0:T(8,128)}) custom-call(s32[8,256]{1,0:T(8,128)} %lists.1.lists_ref, f32[128,128]{1,0:T(8,128)} %bitcast.30, f32[3,1024]{1,0:T(4,128)} %cen_ref.1, f32[3,1024]{1,0:T(4,128)} %nor_ref.1, f32[3,1024]{1,0:T(4,128)} %tan_ref.1, f32[1,1024]{1,0:T(1,128)} %bitcast.34, f32[2,1024]{1,0:T(2,128)} %fwd_ref.1), custom_call_target="tpu_custom_call" | custom-call | tf_op jit(solution)/shard_map/pairs/pallas_call | solution.py:170
  88.2 1.5 copy.22
  89.7 6.6 %all-to-all-start.1 = ((f32[128,1,128]{2,1,0:T(1,128)}), f32[128,1,128]{2,1,0:T(1,128)S(1)}, u32[]{:S(2)}, u32[]{:S(2)}) async-start(f32[128,1,128]{2,1,0:T(1,128)} %bitcast.12), calls=%async_computation.1 | async-start | bytes 131072 | tf_op jit(solution)/shard_map/all_to_all | solution.py:372
  96.3 3.5 %slots.1 = (s32[3,1024]{1,0:T(4,128)}, f32[3,1024]{1,0:T(4,128)}) custom-call(s32[512,128]{1,0:T(8,128)} %bitcast.29, s32[3,1024]{1,0:T(4,128)} %corners_ref.1), custom_call_target="tpu_custom_call" | custom-call | tf_op jit(solution)/shard_map/slots/pallas_call | solution.py:353
  99.8 6.1 %all-to-all-done.1 = f32[128,1,128]{2,1,0:T(1,128)S(1)} async-done(((f32[128,1,128]{2,1,0:T(1,128)}), f32[128,1,128]{2,1,0:T(1,128)S(1)}, u32[]{:S(2)}, u32[]{:S(2)}) %all-to-all-start.1) | async-done | bytes 65568 | tf_op jit(solution)/shard_map/all_to_all | solution.py:372
  105.9 0.2 reduce_sum.9
  106.1 0.1 reshape.55
  106.2 1.4 add_multiply_fusion.values_ref
  107.5 2.7 %buckets.1 = f32[128,256]{1,0:T(8,128)} custom-call(f32[6,1024]{1,0:T(8,128)} %add_multiply_fusion.values_ref, s32[3,1024]{1,0:T(4,128)} %get-tuple-element.10.slots_ref, f32[3,1024]{1,0:T(4,128)} %get-tuple-element.11.ranks_ref), custom_call_target="tpu_custom_call" | custom-call | tf_op jit(solution)/shard_map/buckets/pallas_call | solution.py:353
  110.2 1.7 copy.24
  111.9 4.5 %all-to-all-start.2 = ((f32[128,1,256]{2,1,0:T(1,128)}), f32[128,1,256]{2,1,0:T(1,128)S(1)}, u32[]{:S(2)}, u32[]{:S(2)}) async-start(f32[128,1,256]{2,1,0:T(1,128)} %copy.24), calls=%async_computation.2 | async-start | bytes 262144 | tf_op jit(solution)/shard_map/all_to_all | solution.py:376
  116.4 6.5 %copy.25.modes_ref = f32[300,6,512]{2,1,0:T(8,128)} copy(f32[300,6,512]{2,0,1:T(8,128)} %param.19) | data formatting | bytes 7372800 | tf_op args[9]
  122.9 3.6 %all-to-all-done.2 = f32[128,1,256]{2,1,0:T(1,128)S(1)} async-done(((f32[128,1,256]{2,1,0:T(1,128)}), f32[128,1,256]{2,1,0:T(1,128)S(1)}, u32[]{:S(2)}, u32[]{:S(2)}) %all-to-all-start.2) | async-done | bytes 131104 | tf_op jit(solution)/shard_map/all_to_all | solution.py:376
  126.5 0.7 copy.29
  127.1 5.2 %vertex.1 = (f32[6,512]{1,0:T(8,128)}, f32[1,300]{1,0:T(1,128)}) custom-call(f32[128,256]{1,0:T(8,128)} %bitcast.27, f32[300,6,512]{2,1,0:T(8,128)} %copy.25.modes_ref), custom_call_target="tpu_custom_call" | custom-call | tf_op jit(solution)/shard_map/vertex/pallas_call | solution.py:353
  132.3 0.7 reduce.1
  133.0 63.6 %psum.7 = f32[300]{0:T(512)} all-reduce(f32[300]{0:T(512)S(1)} %reduce.1), channel_id=1, replica_groups=mesh['row'=8,'col'=16] {'row','col'}, use_global_device_ids=true, to_apply=%region_1.2 | all-reduce | flops 300 | bytes 2400 | tf_op jit(solution)/shard_map/psum | solution.py:379
  (2 shorter events, 0.0 us)
Async XLA Ops:
  2.2 55.1 %all-to-all-start = ((f32[8,1,128]{2,1,0:T(1,128)}), f32[8,1,128]{2,1,0:T(1,128)S(1)}, u32[]{:S(2)}, u32[]{:S(2)}) async-start(f32[8,1,128]{2,1,0:T(1,128)} %bitcast.2), calls=%async_computation | async-start | bytes 8192 | tf_op jit(solution)/shard_map/all_to_all | solution.py:368
  57.3 0.6 copy-start
  89.7 16.2 %all-to-all-start.1 = ((f32[128,1,128]{2,1,0:T(1,128)}), f32[128,1,128]{2,1,0:T(1,128)S(1)}, u32[]{:S(2)}, u32[]{:S(2)}) async-start(f32[128,1,128]{2,1,0:T(1,128)} %bitcast.12), calls=%async_computation.1 | async-start | bytes 131072 | tf_op jit(solution)/shard_map/all_to_all | solution.py:372
  111.9 14.5 %all-to-all-start.2 = ((f32[128,1,256]{2,1,0:T(1,128)}), f32[128,1,256]{2,1,0:T(1,128)S(1)}, u32[]{:S(2)}, u32[]{:S(2)}) async-start(f32[128,1,256]{2,1,0:T(1,128)} %copy.24), calls=%async_computation.2 | async-start | bytes 262144 | tf_op jit(solution)/shard_map/all_to_all | solution.py:376

commit v2 on v1

--- a/solution.py
+++ b/solution.py
@@ -206,33 +206,26 @@
 
 
 def make_lists(flags, batches):
-    l0, l1 = iota((128, 128), 0), iota((128, 128), 1)
-    same = (l0 & 7) == (l1 & 7)
-    before = ones_where(same & (l0 < l1)).astype(BF16)
-    same = ones_where(same).astype(BF16)
-    lower = ones_where(iota((8, 8), 0) > iota((8, 8), 1)).astype(BF16)
+    before = ones_where(iota((128, 128), 0) < iota((128, 128), 1)).astype(BF16)
+    tile = iota((8, 128), 0)
     lane = iota((8, 128), 1)
-    tile = iota((8, 128), 0)
-    pick = ones_where(lane == tile).astype(BF16)
     pos = jnp.zeros((8, 128), F32)
-    base = jnp.zeros((8, 128), F32)
+    base = jnp.zeros((8, 1), F32)
     counts = []
     for kind in range(3):
         mask = ones_where(flags == float(kind))
-        mb = mask.astype(BF16)
-        rowtot = dot_nn(mb, same)
-        inside = dot_nn(mb, before) + dot_nn(lower, rowtot.astype(BF16))
-        total = jnp.sum(rowtot, axis=0, keepdims=True) + jnp.zeros((8, 128), F32)
+        inside = dot_nn(mask.astype(BF16), before)
+        total = jnp.sum(mask, axis=1, keepdims=True)
         pos = pos + mask * (inside + base)
         nb = jnp.floor((total + float(batches[kind] - 1)) * (1.0 / batches[kind]))
         base = base + nb * float(batches[kind])
-        counts.append(dot_nt(pick, nb.astype(BF16))[:, 0:1])
+        counts.append(nb)
     posi = pos.astype(jnp.int32)
     slot = iota((256, 128), 0)
     out = jnp.zeros((8, 256), F32)
-    for r in range(8):
-        hit = ones_where(slot == posi[r:r + 1, :]).astype(BF16)
-        value = jnp.where((lane & 7) == tile, ((lane >> 3) * 8 + (r - 128)).astype(F32), 0.0).astype(BF16)
+    for t in range(8):
+        hit = ones_where(slot == posi[t:t + 1, :]).astype(BF16)
+        value = jnp.where(tile == t, (lane - 128).astype(F32), 0.0).astype(BF16)
         out = out + dot_nt(value, hit)
     out = out + 128.0
     wide = iota((8, 256), 1)
@@ -276,22 +269,16 @@
     return jnp.concatenate(rows, axis=0)
 
 
-def fill_buckets(values, slots, ranks):
-    width = 256
-    sub = iota((128, width), 0)
-    rank_of_row = iota((192, width), 0) >> 3
-    send = jnp.zeros((128, 192), F32)
-    for n in range(slots.shape[0]):
-        for cb in range(slots.shape[1] // width):
-            cols = slice(cb * width, (cb + 1) * width)
-            s = slots[n:n + 1, cols]
-            hit = ones_where(sub == (s >> 9)).astype(BF16)
-            eight = jnp.concatenate([values[:, cols], (s & 511).astype(F32), jnp.zeros((1, width), F32)], axis=0)
-            mine = rank_of_row == ranks[n:n + 1, cols].astype(jnp.int32)
-            for part in split3(eight):
-                rhs = jnp.where(mine, jnp.concatenate([part.astype(F32)] * 24, axis=0), 0.0).astype(BF16)
-                send = send + dot_nt(hit, rhs)
-    return jnp.concatenate([send, jnp.zeros((128, 64), F32)], axis=1)
+def bucket_terms(values, slots, ranks):
+    width = values.shape[1]
+    hit = ones_where(iota((128, width), 0) == (slots >> 9)).astype(BF16)
+    mine = (iota((192, width), 0) >> 3) == ranks
+    total = None
+    for part in split3(values):
+        rhs = jnp.where(mine, jnp.concatenate([part.astype(F32)] * 24, axis=0), 0.0).astype(BF16)
+        term = dot_nt(hit, rhs)
+        total = term if total is None else total + term
+    return total
 
 
 def add_up(recv):
@@ -309,74 +296,205 @@
     return total[0:8] + total[8:16] + total[16:24]
 
 
-def lists_kernel(flags_ref, out_ref):
-    out_ref[...] = make_lists(flags_ref[...], BATCHES)
-
-
-def slots_kernel(table_ref, corners_ref, slots_ref, ranks_ref):
-    slots = lookup_slots(table_ref[...], corners_ref[...])
-    slots_ref[...] = slots
-    ranks_ref[...] = patch_ranks(slots >> 9)
-
-
-def bucket_kernel(values_ref, slots_ref, ranks_ref, out_ref):
-    out_ref[...] = fill_buckets(values_ref[...], slots_ref[...], ranks_ref[...])
-
-
-def project(modes_ref, vertex, acc_ref):
-    count = modes_ref.shape[0]
-    step = 10
-
-    def visit(i, _):
-        block = pl.ds(i * step, step)
-        s = sum(modes_ref[block, :, k * 128:(k + 1) * 128] * vertex[None, 0:6, k * 128:(k + 1) * 128] for k in range(4))
-        folded = jnp.sum(s, axis=1)
-        acc_ref[block, :] = folded
-        return 0
-    lax.fori_loop(0, count // step, visit, 0, unroll=False)
-    ones = jnp.ones((8, 128), BF16)
-    return sum(dot_nt(ones, p) for p in split3(acc_ref[...]))
-
-
-def vertex_kernel(recv_ref, modes_ref, vertex_ref, grad_ref, acc_ref):
-    vertex = add_up(recv_ref[...])
-    vertex_ref[...] = vertex[0:6]
-    grad_ref[...] = project(modes_ref, vertex, acc_ref)[0:1]
-
-
 VM = pl.BlockSpec(memory_space=pltpu.VMEM)
 SLAB_DEV = 8
 BATCHES = (8, 4, 4)
-
-
-def simple(kernel, shapes, name, *args, scratch=()):
-    return pl.pallas_call(kernel, out_shape=shapes, in_specs=[VM] * len(args),
-                          out_specs=jax.tree.map(lambda _: VM, shapes), scratch_shapes=scratch, name=name)(*args)
-
-
+N_ROW, N_COL = 8, 16
 S = jax.ShapeDtypeStruct
 I32 = jnp.int32
+DMA = pltpu.SemaphoreType.DMA
+MESH = pl.DeviceIdType.MESH
+
+
+def greet(me):
+    barrier = pltpu.get_barrier_semaphore()
+    for axis, count in (("row", N_ROW), ("col", N_COL)):
+        def signal(k, _, axis=axis, count=count):
+            pl.semaphore_signal(barrier, inc=1, device_id={axis: lax.rem(me[axis] + k, count)}, device_id_type=MESH)
+            return 0
+        lax.fori_loop(1, count, signal, 0)
+    return barrier
+
+
+class Swap:
+    def __init__(self, me, axis, count, piece, slot, sems):
+        self.me, self.count, self.axis = me[axis], count, axis
+        self.piece, self.slot = piece, slot
+        self.send_sem, self.recv_sem = sems
+
+    def copy(self, peer, slot):
+        return pltpu.make_async_remote_copy(
+            src_ref=self.piece(peer), dst_ref=self.slot(slot), send_sem=self.send_sem.at[peer], recv_sem=self.recv_sem.at[slot],
+            device_id={self.axis: peer}, device_id_type=MESH)
+
+    def each(self, act):
+        def visit(k, _):
+            act(lax.rem(self.me + k, self.count))
+            return 0
+        lax.fori_loop(1, self.count, visit, 0)
+
+    def start(self):
+        self.each(lambda peer: self.copy(peer, self.me).start())
+
+    def receive(self):
+        self.each(lambda peer: self.copy(peer, peer).wait_recv())
+
+    def drain(self):
+        self.each(lambda peer: self.copy(peer, peer).wait_send())
+
+
+def swap_sems(n):
+    return [DMA((n,)), DMA((n,))]
+
+
+def gather_kernel(cen_ref, adj_ref, flags_ref, table_ref, corners_ref, rows_out, lists_out, slots_out, ranks_out,
+                  own, rowblk, rowall, flagall, fs, fr, cs, cr, rs, rr):
+    me = {"row": lax.axis_index("row"), "col": lax.axis_index("col")}
+    barrier = greet(me)
+    lane = iota((1, 128), 1)
+    packed = jnp.zeros((1, 128), F32)
+    for q in range(5):
+        line = cen_ref[q:q + 1, 0:128] if q < 3 else adj_ref[q - 3:q - 2, 0:128]
+        if q:
+            line = pltpu.roll(line, 8 * q, 1)
+        packed = jnp.where((lane >> 3) == q, line, packed)
+    own[...] = packed
+    rowblk[pl.ds(me["col"], 1), :] = packed
+    flagall[me["row"]] = flags_ref[me["row"]]
+    pl.semaphore_wait(barrier, N_ROW + N_COL - 2)
+    flag_swap = Swap(me, "row", N_ROW, lambda peer: flags_ref.at[peer], lambda slot: flagall.at[slot], (fs, fr))
+    col_swap = Swap(me, "col", N_COL, lambda peer: own, lambda slot: rowblk.at[pl.ds(slot, 1), :], (cs, cr))
+    row_swap = Swap(me, "row", N_ROW, lambda peer: rowblk, lambda slot: rowall.at[slot], (rs, rr))
+    col_swap.start()
+    flag_swap.start()
+    slots = lookup_slots(table_ref[...], corners_ref[...])
+    slots_out[...] = slots
+    col_swap.receive()
+    row_swap.start()
+    rowall[me["row"]] = rowblk[...]
+    ranks_out[...] = patch_ranks(slots >> 9).astype(I32)
+    flag_swap.receive()
+    flags = jnp.concatenate([flagall[r] for r in range(N_ROW)], axis=1).astype(F32)
+    lists_out[...] = make_lists(flags, BATCHES)
+    row_swap.receive()
+    for r in range(N_ROW):
+        rows_out[r * N_COL:(r + 1) * N_COL, :] = rowall[r]
+    for swap in (col_swap, flag_swap, row_swap):
+        swap.drain()
+
+
+def project(modes_ref, vertex, acc_ref):
+    total = None
+    for comp in range(6):
+        for k in range(4):
+            lanes = slice(k * 128, (k + 1) * 128)
+            term = modes_ref[comp, :, lanes] * vertex[comp:comp + 1, lanes]
+            total = term if total is None else total + term
+    acc_ref[...] = jnp.zeros(acc_ref.shape, F32)
+    acc_ref[0:total.shape[0], :] = total
+    ones = jnp.ones((8, 128), BF16)
+    return sum(dot_nt(ones, p) for p in split3(acc_ref[...]))
+
+
+def finish_kernel(col_ref, row_ref, slots_ref, ranks_ref, modes_hbm, vertex_out, grad_out,
+                  modes, part16, sum16, own16, send, mid, stage, recv, acc, grad, grad8, mid_grad, grad16,
+                  msem, a0, a1, b0, b1, c0, c1, d0, d1, e0, e1, f0, f1):
+    me = {"row": lax.axis_index("row"), "col": lax.axis_index("col")}
+    r, c = me["row"], me["col"]
+    barrier = greet(me)
+    fetch = pltpu.make_async_copy(modes_hbm, modes, msem)
+    fetch.start()
+    pl.semaphore_wait(barrier, N_ROW + N_COL - 2)
+
+    def block(ref, i):
+        return ref.at[pl.ds(pl.multiple_of(i * N_COL, N_COL), N_COL), :]
+
+    def halves(ref, i):
+        return ref.at[:, pl.ds(pl.multiple_of(i * N_COL, N_COL), N_COL), :]
+
+    swap_a = Swap(me, "row", N_ROW, lambda peer: block(row_ref, peer), lambda slot: part16.at[slot], (a0, a1))
+    swap_b = Swap(me, "col", N_COL, lambda peer: sum16.at[pl.ds(peer, 1), :], lambda slot: own16.at[pl.ds(slot, 1), :], (b0, b1))
+    swap_c = Swap(me, "row", N_ROW, lambda peer: halves(send, peer), lambda slot: halves(mid, slot), (c0, c1))
+    swap_d = Swap(me, "col", N_COL, lambda peer: stage.at[peer], lambda slot: recv.at[slot], (d0, d1))
+    swap_e = Swap(me, "row", N_ROW, lambda peer: grad, lambda slot: grad8.at[slot], (e0, e1))
+    swap_f = Swap(me, "col", N_COL, lambda peer: mid_grad, lambda slot: grad16.at[slot], (f0, f1))
+
+    swap_a.start()
+    part16[r] = block(row_ref, r)[...]
+    width = 256
+    third = 1.0 / 3.0
+    total = jnp.zeros((128, 192), F32)
+    for n in range(3):
+        for cb in range(col_ref.shape[1] // width):
+            cols = slice(cb * width, (cb + 1) * width)
+            s = slots_ref[n:n + 1, cols]
+            eight = jnp.concatenate([col_ref[:, cols] * third, (s & 511).astype(F32), jnp.zeros((1, width), F32)], axis=0)
+            total = total + bucket_terms(eight, s, ranks_ref[n:n + 1, cols])
+        if n == 0:
+            swap_a.receive()
+            sum16[...] = sum(part16[i] for i in range(N_ROW))
+            swap_b.start()
+            own16[pl.ds(c, 1), :] = sum16[pl.ds(c, 1), :]
+    swap_b.receive()
+    own = jnp.sum(own16[...], axis=0, keepdims=True) * third
+    lane = iota((1, 128), 1)
+    lines = [jnp.where(lane < 8, own if q == 0 else pltpu.roll(own, 128 - 8 * q, 1), 0.0) for q in range(3)]
+    extra = jnp.concatenate(lines + [jnp.zeros((5, 128), F32)], axis=0)
+    for n in range(3):
+        total = total + bucket_terms(extra, slots_ref[n:n + 1, 0:128], ranks_ref[n:n + 1, 0:128])
+    send[0] = total[:, 0:128]
+    send[1] = jnp.concatenate([total[:, 128:192], jnp.zeros((128, 64), F32)], axis=1)
+    swap_c.start()
+    halves(mid, r)[...] = halves(send, r)[...]
+    swap_c.receive()
+    for i in range(N_COL):
+        for half in range(2):
+            stage[i, :, half * 128:(half + 1) * 128] = mid[half, pl.ds(i, N_ROW, stride=N_COL), :]
+    swap_d.start()
+    recv[c] = stage[c]
+    swap_d.receive()
+    vertex = add_up(recv[...].reshape(128, 256))
+    vertex_out[...] = vertex[0:6]
+    fetch.wait()
+    grad[...] = project(modes, vertex, acc)[0:1]
+    swap_e.start()
+    grad8[r] = grad[...]
+    swap_e.receive()
+    mid_grad[...] = sum(grad8[i] for i in range(N_ROW))
+    swap_f.start()
+    grad16[c] = mid_grad[...]
+    swap_f.receive()
+    grad_out[...] = sum(grad16[i] for i in range(N_COL))[:, 0:grad_out.shape[1]]
+    for swap in (swap_a, swap_b, swap_c, swap_d, swap_e, swap_f):
+        swap.drain()
 
 
 def body(centroid, normals, tangent, element_area, forward_field, adjoint_field, corners, slot_map, quad_order, morph_modes):
     el = centroid.shape[1]
-    slab = jnp.concatenate([centroid[:, :8], adjoint_field[:, :8]], axis=0).reshape(1, 40)
-    slab = jnp.pad(slab, ((0, 0), (0, 88)))
-    rows = lax.all_gather(slab, ("row", "col"), axis=0, tiled=True)
-    rows = rows.reshape(8, 16, 128).transpose(1, 0, 2).reshape(128, 128)
-    flags = quad_order[:, :, 0, :].transpose(1, 0, 2).reshape(8, 128).astype(F32)
-    flags = lax.all_to_all(flags, "row", 0, 0, tiled=True)
-    lists = simple(lists_kernel, S((8, 256), I32), "lists", flags)
+    modes_t = jnp.transpose(morph_modes, (1, 0, 2))
+    flags = jnp.transpose(quad_order[:, :, 0, :], (1, 2, 0))
+    whole = pl.BlockSpec(memory_space=pltpu.VMEM)
+    rows, lists, slots, ranks = pl.pallas_call(
+        gather_kernel,
+        out_shape=(S((128, 128), F32), S((8, 256), I32), S((3, el), I32), S((3, el), I32)),
+        in_specs=[whole] * 5, out_specs=(whole,) * 4,
+        scratch_shapes=[pltpu.VMEM((1, 128), F32), pltpu.VMEM((16, 128), F32), pltpu.VMEM((8, 16, 128), F32),
+                        pltpu.VMEM((8, 8, 16), I32)] + swap_sems(8) + swap_sems(16) + swap_sems(8),
+        compiler_params=pltpu.CompilerParams(collective_id=0, has_side_effects=True), name="gather",
+    )(centroid, adjoint_field, flags, slot_map.reshape(512, 128), corners)
     col_part, row_part = pair_call(lists, rows, centroid, normals, tangent, element_area[None, :], forward_field, BATCHES)
-    row_part = row_part.reshape(16, 8, 128).transpose(1, 0, 2).reshape(128, 128)
-    own = jnp.sum(lax.all_to_all(row_part, ("row", "col"), 0, 0, tiled=True), axis=0)[:24].reshape(3, 8)
-    element_part = col_part + jnp.pad(own, ((0, 3), (0, el - 8)))
-    slots, ranks = simple(slots_kernel, (S((3, el), I32), S((3, el), F32)), "slots", slot_map.reshape(512, 128), corners)
-    send = simple(bucket_kernel, S((128, 256), F32), "buckets", element_part / 3.0, slots, ranks)
-    recv = lax.all_to_all(send, ("row", "col"), 0, 0, tiled=True)
-    vertex, grad = simple(vertex_kernel, (S((6, 512), F32), S((1, 300), F32)), "vertex", recv, morph_modes,
-                          scratch=[pltpu.VMEM((300, 128), F32)])
-    return vertex, lax.psum(grad[0], ("row", "col"))
+    vertex, grad = pl.pallas_call(
+        finish_kernel,
+        out_shape=(S((6, 512), F32), S((1, 300), F32)),
+        in_specs=[whole] * 4 + [pl.BlockSpec(memory_space=pl.ANY)], out_specs=(whole, whole),
+        scratch_shapes=[pltpu.VMEM((6, 300, 512), F32), pltpu.VMEM((8, 16, 128), F32), pltpu.VMEM((16, 128), F32),
+                        pltpu.VMEM((16, 128), F32), pltpu.VMEM((2, 128, 128), F32), pltpu.VMEM((2, 128, 128), F32),
+                        pltpu.VMEM((16, 8, 256), F32), pltpu.VMEM((16, 8, 256), F32), pltpu.VMEM((384, 128), F32),
+                        pltpu.VMEM((1, 384), F32), pltpu.VMEM((8, 1, 384), F32), pltpu.VMEM((1, 384), F32),
+                        pltpu.VMEM((16, 1, 384), F32), DMA] + (swap_sems(8) + swap_sems(16)) * 3,
+        compiler_params=pltpu.CompilerParams(collective_id=1, has_side_effects=True), name="finish",
+    )(col_part, row_part, slots, ranks, modes_t)
+    return vertex, grad[0]
 
 
 def solution(mesh):

time: 197 us -> 84.8 us (0.43)
  blocking collectives: 111 us -> 0 us
  Pallas kernels: 41.7 us -> 81.2 us
  starting transfers between devices: 16.9 us -> 0 us
  local copies, waits for them, and re-layouts: 13.8 us -> 1.32 us
  waiting for transfers between devices: 9.71 us -> 0 us
    psum x1 -> x0, blocking collectives: 63.6 us -> none  [body(): return (vertex, lax.psum(grad[0], ('row', 'col')))]
    all_gather x1 -> x0, blocking collectives: 47.2 us -> none  [body(): rows = lax.all_gather(slab, ('row', 'col'), axis=0, tiled=True)]
    pallas_call x4 -> x2, Pallas kernels: 13.5 us -> 52.9 us  [the longest x1 34 us: body(): pl.pallas_call(finish_kernel, out_shape=(S((6, 512), F32), S((1, 300), F3...]
    all_to_all x3 -> x0, starting transfers between devices: 16.9 us -> none  [the longest x1 6.65 us: body(): lax.all_to_all(row_part, ('row', 'col'), 0, 0, tiled=True)]
    all_to_all x3 -> x0, waiting for transfers between devices: 9.71 us -> none  [the longest x1 6.13 us: body(): lax.all_to_all(row_part, ('row', 'col'), 0, 0, tiled=True)]
    unnamed x5 -> x1, local copies, waits for them, and re-layouts: 7.72 us -> 1.32 us
    reshape x4 -> x0, local copies, waits for them, and re-layouts: 2.26 us -> none  [the longest x1 1.46 us: body(): row_part = row_part.reshape(16, 8, 128).transpose(1, 0, 2).reshape(128, 128)]
  transfers between devices with their start and end apart: 3 -> 0, of which waited for: 2 -> 0; matrix products, arithmetic and copies ran while one was open for 4% -> 0% of each run, Pallas kernels for 2% -> 0%
where the time goes in v2:
time: 84.8 us; the launch traced here: 84.5 us
  Pallas kernels  81.2 us (96%)
  local copies, waits for them, and re-layouts  1.32 us (2%)
  other arithmetic  1.28 us (2%)
    pallas_call x1, Pallas kernels, body(): pl.pallas_call(finish_kernel, out_shape=(S((6, 512), F32), S((1, 300), F3...  34 us
    pallas_call x1, Pallas kernels, pair_call(): pl.pallas_call(functools.partial(pair_kernel, batches, groups), out_shape...  28.4 us
    pallas_call x1, Pallas kernels, body(): pl.pallas_call(gather_kernel, out_shape=(S((128, 128), F32), S((8, 256),...  18.9 us

profile of v2, /device:TPU:1, one launch (start us, length us, event | category | flops | bytes accessed | tf_op | source)
XLA Modules:
  0.0 84.5 jit_solution(7367135151355389930)
XLA Ops:
  0.6 18.9 %gather.1 = (f32[128,128]{1,0:T(8,128)}, s32[8,256]{1,0:T(8,128)}, s32[3,1024]{1,0:T(4,128)}, s32[3,1024]{1,0:T(4,128)}) custom-call(f32[3,1024]{1,0:T(4,128)} %cen_ref.3, f32[2,1024]{1,0:T(2,128)} %adj_ref.1, s32[8,8,16]{2,1,0:T(8,128)} %bitcast.8, s32[512,128]{1,0:T(8,128)} %bitcast.7, s32[3,1024]{1,0:T(4,128)} %corners_ref.1), custom_call_target="tpu_custom_call" | custom-call | tf_op jit(solution)/shard_map/gather/pallas_call | solution.py:477
  19.5 28.4 %pairs.1 = (f32[6,1024]{1,0:T(8,128)}, f32[128,128]{1,0:T(8,128)}) custom-call(s32[8,256]{1,0:T(8,128)} %get-tuple-element.10.lists_ref, f32[128,128]{1,0:T(8,128)} %get-tuple-element.11.rows_ref, f32[3,1024]{1,0:T(4,128)} %cen_ref.3, f32[3,1024]{1,0:T(4,128)} %nor_ref.1, f32[3,1024]{1,0:T(4,128)} %tan_ref.1, f32[1,1024]{1,0:T(1,128)} %bitcast.9, ...), custom_call_target="tpu_custom_call" | custom-call | tf_op jit(solution)/shard_map/pairs/pallas_call | solution.py:170
  47.9 34.0 %finish.1 = (f32[6,512]{1,0:T(8,128)}, f32[1,300]{1,0:T(1,128)}) custom-call(f32[6,1024]{1,0:T(8,128)} %get-tuple-element.12.col_ref, f32[128,128]{1,0:T(8,128)} %get-tuple-element.13.row_ref, s32[3,1024]{1,0:T(4,128)} %get-tuple-element.14.slots_ref, s32[3,1024]{1,0:T(4,128)} %get-tuple-element.15.ranks_ref, f32[6,300,512]{2,1,0:T(8,128)} %bitcast.6), custom_call_target="tpu_custom_call" | custom-call | tf_op jit(solution)/shard_map/finish/pallas_call | solution.py:486
  81.9 1.3 %reduce = f32[300]{0:T(512)} reduce(f32[1,300]{1,0:T(1,128)} %get-tuple-element.17, f32[]{:T(128)} %constant.1), dimensions={0}, to_apply=%get-tuple-element.17.reduce_sub_computation | reduce | bytes 2404 | tf_op jit(solution)/shard_map/finish/pallas_call | solution.py:486
  83.2 1.3 %copy.13 = f32[6,512]{1,0:T(8,128)} copy(f32[6,512]{1,0:T(8,128)} %get-tuple-element.20) | data formatting | bytes 24576

commit v3 on v2

--- a/solution.py
+++ b/solution.py
@@ -159,8 +159,8 @@
         for q in range(3):
             s = jnp.sum(racc[g, q], axis=1, keepdims=True)
             outs[q] = jnp.where(lane == g, s, outs[q])
-    full = jnp.concatenate(outs + [jnp.zeros((104, 128), F32)], axis=0)
-    row_out[...] = jnp.transpose(full)
+    for q in range(3):
+        row_out[q * 8:(q + 1) * 8, :] = outs[q]
 
 
 def pair_call(lists, rows, cen, nor, tan, area, fwd, batches=(8, 4, 4)):
@@ -169,7 +169,7 @@
     vm = pl.BlockSpec(memory_space=pltpu.VMEM)
     return pl.pallas_call(
         functools.partial(pair_kernel, batches, groups),
-        out_shape=(jax.ShapeDtypeStruct((6, el), F32), jax.ShapeDtypeStruct((128, 128), F32)),
+        out_shape=(jax.ShapeDtypeStruct((6, el), F32), jax.ShapeDtypeStruct((24, 128), F32)),
         in_specs=[pl.BlockSpec(memory_space=pltpu.SMEM)] + [vm] * 6,
         out_specs=(vm, vm),
         scratch_shapes=[pltpu.VMEM((groups + 1, 5, 8, 128), F32), pltpu.VMEM((groups + 1, 3, 8, 128), F32),
@@ -225,7 +225,7 @@
     out = jnp.zeros((8, 256), F32)
     for t in range(8):
         hit = ones_where(slot == posi[t:t + 1, :]).astype(BF16)
-        value = jnp.where(tile == t, (lane - 128).astype(F32), 0.0).astype(BF16)
+        value = jnp.where(tile == t, (((lane & 15) << 3) + (lane >> 4) - 128).astype(F32), 0.0).astype(BF16)
         out = out + dot_nt(value, hit)
     out = out + 128.0
     wide = iota((8, 256), 1)
@@ -281,14 +281,20 @@
     return total
 
 
-def add_up(recv):
+def add_up(recv, rows):
     turned = jnp.transpose(recv)
     sub = iota((512, 128), 0).astype(F32)
+    row8 = iota((8, 128), 0)
+    row8f = row8.astype(F32)
     total = jnp.zeros((24, 512), F32)
     for pair in range(12):
         parts, hits = [], []
         for q in (2 * pair, 2 * pair + 1):
             eight = turned[q * 8:(q + 1) * 8, :]
+            mine = ones_where(row8f == eight[7:8, :])
+            for comp in range(3):
+                gain = jnp.sum(mine * rows[comp * 8:(comp + 1) * 8], axis=0, keepdims=True)
+                eight = eight + jnp.where(row8 == comp, gain, 0.0)
             hits.append(ones_where(sub == eight[6:7, :]).astype(BF16))
             parts.append(jnp.concatenate([p.astype(F32) for p in split3(eight)], axis=0))
         lhs = jnp.concatenate(parts, axis=1).astype(BF16)
@@ -347,7 +353,7 @@
     return [DMA((n,)), DMA((n,))]
 
 
-def gather_kernel(cen_ref, adj_ref, flags_ref, table_ref, corners_ref, rows_out, lists_out, slots_out, ranks_out,
+def gather_kernel(cen_ref, adj_ref, flags_ref, table_ref, corners_ref, rows_out, lists_out, codes_out,
                   own, rowblk, rowall, flagall, fs, fr, cs, cr, rs, rr):
     me = {"row": lax.axis_index("row"), "col": lax.axis_index("col")}
     barrier = greet(me)
@@ -361,24 +367,24 @@
     own[...] = packed
     rowblk[pl.ds(me["col"], 1), :] = packed
     flagall[me["row"]] = flags_ref[me["row"]]
+    slots = lookup_slots(table_ref[...], corners_ref[...])
+    codes_out[...] = slots * 32 + patch_ranks(slots >> 9).astype(I32)
     pl.semaphore_wait(barrier, N_ROW + N_COL - 2)
     flag_swap = Swap(me, "row", N_ROW, lambda peer: flags_ref.at[peer], lambda slot: flagall.at[slot], (fs, fr))
     col_swap = Swap(me, "col", N_COL, lambda peer: own, lambda slot: rowblk.at[pl.ds(slot, 1), :], (cs, cr))
-    row_swap = Swap(me, "row", N_ROW, lambda peer: rowblk, lambda slot: rowall.at[slot], (rs, rr))
+    row_swap = Swap(me, "row", N_ROW, lambda peer: rowblk,
+                    lambda slot: rowall.at[pl.ds(pl.multiple_of(slot * N_COL, N_COL), N_COL), :], (rs, rr))
     col_swap.start()
     flag_swap.start()
-    slots = lookup_slots(table_ref[...], corners_ref[...])
-    slots_out[...] = slots
-    col_swap.receive()
-    row_swap.start()
-    rowall[me["row"]] = rowblk[...]
-    ranks_out[...] = patch_ranks(slots >> 9).astype(I32)
     flag_swap.receive()
     flags = jnp.concatenate([flagall[r] for r in range(N_ROW)], axis=1).astype(F32)
     lists_out[...] = make_lists(flags, BATCHES)
+    col_swap.receive()
+    row_swap.start()
+    rowall[pl.ds(pl.multiple_of(me["row"] * N_COL, N_COL), N_COL), :] = rowblk[...]
     row_swap.receive()
-    for r in range(N_ROW):
-        rows_out[r * N_COL:(r + 1) * N_COL, :] = rowall[r]
+    for c in range(N_COL):
+        rows_out[c * N_ROW:(c + 1) * N_ROW, :] = rowall[pl.ds(c, N_ROW, stride=N_COL), :]
     for swap in (col_swap, flag_swap, row_swap):
         swap.drain()
 
@@ -396,64 +402,57 @@
     return sum(dot_nt(ones, p) for p in split3(acc_ref[...]))
 
 
-def finish_kernel(col_ref, row_ref, slots_ref, ranks_ref, modes_hbm, vertex_out, grad_out,
-                  modes, part16, sum16, own16, send, mid, stage, recv, acc, grad, grad8, mid_grad, grad16,
+def finish_kernel(col_ref, row_ref, codes_ref, modes_hbm, vertex_out, grad_out,
+                  modes, part8, sumrow, part16, send, mid, stage, recv, acc, grad, grad8, mid_grad, grad16,
                   msem, a0, a1, b0, b1, c0, c1, d0, d1, e0, e1, f0, f1):
     me = {"row": lax.axis_index("row"), "col": lax.axis_index("col")}
     r, c = me["row"], me["col"]
     barrier = greet(me)
     fetch = pltpu.make_async_copy(modes_hbm, modes, msem)
     fetch.start()
-    pl.semaphore_wait(barrier, N_ROW + N_COL - 2)
-
-    def block(ref, i):
-        return ref.at[pl.ds(pl.multiple_of(i * N_COL, N_COL), N_COL), :]
 
     def halves(ref, i):
         return ref.at[:, pl.ds(pl.multiple_of(i * N_COL, N_COL), N_COL), :]
 
-    swap_a = Swap(me, "row", N_ROW, lambda peer: block(row_ref, peer), lambda slot: part16.at[slot], (a0, a1))
-    swap_b = Swap(me, "col", N_COL, lambda peer: sum16.at[pl.ds(peer, 1), :], lambda slot: own16.at[pl.ds(slot, 1), :], (b0, b1))
+    swap_a = Swap(me, "row", N_ROW, lambda peer: row_ref, lambda slot: part8.at[slot], (a0, a1))
+    swap_b = Swap(me, "col", N_COL, lambda peer: sumrow, lambda slot: part16.at[slot], (b0, b1))
     swap_c = Swap(me, "row", N_ROW, lambda peer: halves(send, peer), lambda slot: halves(mid, slot), (c0, c1))
     swap_d = Swap(me, "col", N_COL, lambda peer: stage.at[peer], lambda slot: recv.at[slot], (d0, d1))
     swap_e = Swap(me, "row", N_ROW, lambda peer: grad, lambda slot: grad8.at[slot], (e0, e1))
     swap_f = Swap(me, "col", N_COL, lambda peer: mid_grad, lambda slot: grad16.at[slot], (f0, f1))
 
-    swap_a.start()
-    part16[r] = block(row_ref, r)[...]
     width = 256
     third = 1.0 / 3.0
     total = jnp.zeros((128, 192), F32)
     for n in range(3):
         for cb in range(col_ref.shape[1] // width):
             cols = slice(cb * width, (cb + 1) * width)
-            s = slots_ref[n:n + 1, cols]
-            eight = jnp.concatenate([col_ref[:, cols] * third, (s & 511).astype(F32), jnp.zeros((1, width), F32)], axis=0)
-            total = total + bucket_terms(eight, s, ranks_ref[n:n + 1, cols])
-        if n == 0:
-            swap_a.receive()
-            sum16[...] = sum(part16[i] for i in range(N_ROW))
-            swap_b.start()
-            own16[pl.ds(c, 1), :] = sum16[pl.ds(c, 1), :]
-    swap_b.receive()
-    own = jnp.sum(own16[...], axis=0, keepdims=True) * third
-    lane = iota((1, 128), 1)
-    lines = [jnp.where(lane < 8, own if q == 0 else pltpu.roll(own, 128 - 8 * q, 1), 0.0) for q in range(3)]
-    extra = jnp.concatenate(lines + [jnp.zeros((5, 128), F32)], axis=0)
-    for n in range(3):
-        total = total + bucket_terms(extra, slots_ref[n:n + 1, 0:128], ranks_ref[n:n + 1, 0:128])
+            code = codes_ref[n:n + 1, cols]
+            slots = code >> 5
+            element = jnp.minimum(iota((1, width), 1) + cb * width, SLAB_DEV).astype(F32)
+            eight = jnp.concatenate([col_ref[:, cols] * third, (slots & 511).astype(F32), element], axis=0)
+            total = total + bucket_terms(eight, slots, code & 31)
     send[0] = total[:, 0:128]
     send[1] = jnp.concatenate([total[:, 128:192], jnp.zeros((128, 64), F32)], axis=1)
+    pl.semaphore_wait(barrier, N_ROW + N_COL - 2)
+    swap_a.start()
     swap_c.start()
+    part8[r] = row_ref[...]
     halves(mid, r)[...] = halves(send, r)[...]
+    swap_a.receive()
+    sumrow[...] = sum(part8[i] for i in range(N_ROW)) * third
+    swap_b.start()
+    part16[c] = sumrow[...]
     swap_c.receive()
     for i in range(N_COL):
         for half in range(2):
             stage[i, :, half * 128:(half + 1) * 128] = mid[half, pl.ds(i, N_ROW, stride=N_COL), :]
     swap_d.start()
     recv[c] = stage[c]
+    swap_b.receive()
+    rows = sum(part16[i] for i in range(N_COL))
     swap_d.receive()
-    vertex = add_up(recv[...].reshape(128, 256))
+    vertex = add_up(recv[...].reshape(128, 256), rows)
     vertex_out[...] = vertex[0:6]
     fetch.wait()
     grad[...] = project(modes, vertex, acc)[0:1]
@@ -464,37 +463,42 @@
     swap_f.start()
     grad16[c] = mid_grad[...]
     swap_f.receive()
-    grad_out[...] = sum(grad16[i] for i in range(N_COL))[:, 0:grad_out.shape[1]]
+    grad_out[...] = sum(grad16[i] for i in range(N_COL))
     for swap in (swap_a, swap_b, swap_c, swap_d, swap_e, swap_f):
         swap.drain()
+
+
+def emit_kernel(vertex_ref, grad_ref, vertex_out, grad_out):
+    vertex_out[...] = vertex_ref[...]
+    grad_out[...] = grad_ref[...].reshape(grad_ref.shape[1])[0:grad_out.shape[0]]
 
 
 def body(centroid, normals, tangent, element_area, forward_field, adjoint_field, corners, slot_map, quad_order, morph_modes):
     el = centroid.shape[1]
     modes_t = jnp.transpose(morph_modes, (1, 0, 2))
     flags = jnp.transpose(quad_order[:, :, 0, :], (1, 2, 0))
-    whole = pl.BlockSpec(memory_space=pltpu.VMEM)
-    rows, lists, slots, ranks = pl.pallas_call(
+    rows, lists, codes = pl.pallas_call(
         gather_kernel,
-        out_shape=(S((128, 128), F32), S((8, 256), I32), S((3, el), I32), S((3, el), I32)),
-        in_specs=[whole] * 5, out_specs=(whole,) * 4,
-        scratch_shapes=[pltpu.VMEM((1, 128), F32), pltpu.VMEM((16, 128), F32), pltpu.VMEM((8, 16, 128), F32),
+        out_shape=(S((128, 128), F32), S((8, 256), I32), S((3, el), I32)),
+        in_specs=[VM] * 5, out_specs=(VM,) * 3,
+        scratch_shapes=[pltpu.VMEM((1, 128), F32), pltpu.VMEM((16, 128), F32), pltpu.VMEM((128, 128), F32),
                         pltpu.VMEM((8, 8, 16), I32)] + swap_sems(8) + swap_sems(16) + swap_sems(8),
         compiler_params=pltpu.CompilerParams(collective_id=0, has_side_effects=True), name="gather",
     )(centroid, adjoint_field, flags, slot_map.reshape(512, 128), corners)
     col_part, row_part = pair_call(lists, rows, centroid, normals, tangent, element_area[None, :], forward_field, BATCHES)
     vertex, grad = pl.pallas_call(
         finish_kernel,
-        out_shape=(S((6, 512), F32), S((1, 300), F32)),
-        in_specs=[whole] * 4 + [pl.BlockSpec(memory_space=pl.ANY)], out_specs=(whole, whole),
-        scratch_shapes=[pltpu.VMEM((6, 300, 512), F32), pltpu.VMEM((8, 16, 128), F32), pltpu.VMEM((16, 128), F32),
-                        pltpu.VMEM((16, 128), F32), pltpu.VMEM((2, 128, 128), F32), pltpu.VMEM((2, 128, 128), F32),
+        out_shape=(S((6, 512), F32), S((1, 384), F32)),
+        in_specs=[VM] * 3 + [pl.BlockSpec(memory_space=pl.ANY)], out_specs=(VM, VM),
+        scratch_shapes=[pltpu.VMEM((6, 300, 512), F32), pltpu.VMEM((8, 24, 128), F32), pltpu.VMEM((24, 128), F32),
+                        pltpu.VMEM((16, 24, 128), F32), pltpu.VMEM((2, 128, 128), F32), pltpu.VMEM((2, 128, 128), F32),
                         pltpu.VMEM((16, 8, 256), F32), pltpu.VMEM((16, 8, 256), F32), pltpu.VMEM((384, 128), F32),
                         pltpu.VMEM((1, 384), F32), pltpu.VMEM((8, 1, 384), F32), pltpu.VMEM((1, 384), F32),
                         pltpu.VMEM((16, 1, 384), F32), DMA] + (swap_sems(8) + swap_sems(16)) * 3,
         compiler_params=pltpu.CompilerParams(collective_id=1, has_side_effects=True), name="finish",
-    )(col_part, row_part, slots, ranks, modes_t)
-    return vertex, grad[0]
+    )(col_part, row_part, codes, modes_t)
+    return pl.pallas_call(emit_kernel, out_shape=(S((6, 512), F32), S((300,), F32)), in_specs=[VM] * 2, out_specs=(VM, VM),
+                          name="emit")(vertex, grad)
 
 
 def solution(mesh):

time: 84.8 us -> 77.8 us (0.917)
  Pallas kernels: 81.2 us -> 77.1 us
  local copies, waits for them, and re-layouts: 1.32 us -> 0 us
  other arithmetic: 1.28 us -> 0 us
    pallas_call x1 -> x2, Pallas kernels: 34 us -> 29.9 us  [the longest x1 28.6 us: body(): pl.pallas_call(finish_kernel, out_shape=(S((6, 512), F32), S((1, 384), F3...]
    unnamed x1 -> x0, local copies, waits for them, and re-layouts: 1.32 us -> none
    pallas_call x1 -> x0, other arithmetic: 1.28 us -> none  [body(): pl.pallas_call(finish_kernel, out_shape=(S((6, 512), F32), S((1, 300), F3...]
where the time goes in v3:
time: 77.8 us; the launch traced here: 77.7 us
  Pallas kernels  77.1 us (99%)
    pallas_call x1, Pallas kernels, body(): pl.pallas_call(finish_kernel, out_shape=(S((6, 512), F32), S((1, 384), F3...  28.6 us
    pallas_call x1, Pallas kernels, pair_call(): pl.pallas_call(functools.partial(pair_kernel, batches, groups), out_shape...  28.2 us
    pallas_call x1, Pallas kernels, body(): pl.pallas_call(gather_kernel, out_shape=(S((128, 128), F32), S((8, 256),...  18.9 us

profile of v3, /device:TPU:1, one launch (start us, length us, event | category | flops | bytes accessed | tf_op | source)
XLA Modules:
  0.0 77.7 jit_solution(15699000741950553778)
XLA Ops:
  0.6 18.9 %gather.1 = (f32[128,128]{1,0:T(8,128)}, s32[8,256]{1,0:T(8,128)}, s32[3,1024]{1,0:T(4,128)}) custom-call(f32[3,1024]{1,0:T(4,128)} %cen_ref.3, f32[2,1024]{1,0:T(2,128)} %adj_ref.1, s32[8,8,16]{2,1,0:T(8,128)} %bitcast.8, s32[512,128]{1,0:T(8,128)} %bitcast.7, s32[3,1024]{1,0:T(4,128)} %corners_ref.1), custom_call_target="tpu_custom_call" | custom-call | tf_op jit(solution)/shard_map/gather/pallas_call | solution.py:480
  19.6 28.2 %pairs.1 = (f32[6,1024]{1,0:T(8,128)}, f32[24,128]{1,0:T(8,128)}) custom-call(s32[8,256]{1,0:T(8,128)} %get-tuple-element.9.lists_ref, f32[128,128]{1,0:T(8,128)} %get-tuple-element.10.rows_ref, f32[3,1024]{1,0:T(4,128)} %cen_ref.3, f32[3,1024]{1,0:T(4,128)} %nor_ref.1, f32[3,1024]{1,0:T(4,128)} %tan_ref.1, f32[1,1024]{1,0:T(1,128)} %bitcast.9, ...), custom_call_target="tpu_custom_call" | custom-call | tf_op jit(solution)/shard_map/pairs/pallas_call | solution.py:170
  47.8 28.6 %finish.1 = (f32[6,512]{1,0:T(8,128)}, f32[1,384]{1,0:T(1,128)}) custom-call(f32[6,1024]{1,0:T(8,128)} %get-tuple-element.11.col_ref, f32[24,128]{1,0:T(8,128)} %get-tuple-element.12.row_ref, s32[3,1024]{1,0:T(4,128)} %get-tuple-element.13.codes_ref, f32[6,300,512]{2,1,0:T(8,128)} %bitcast.6), custom_call_target="tpu_custom_call" | custom-call | tf_op jit(solution)/shard_map/finish/pallas_call | solution.py:489
  76.4 1.3 %emit.1 = (f32[6,512]{1,0:T(8,128)}, f32[300]{0:T(512)}) custom-call(f32[6,512]{1,0:T(8,128)} %get-tuple-element.14.vertex_ref, f32[1,384]{1,0:T(1,128)} %get-tuple-element.15.grad_ref), custom_call_target="tpu_custom_call" | custom-call | tf_op jit(solution)/shard_map/emit/pallas_call | solution.py:500

commit v4 on v3

--- a/solution.py
+++ b/solution.py
@@ -22,7 +22,7 @@
     inv = lax.rsqrt(r2)
     phi = r2 * inv
     turn = phi * INV_TURN
-    frac = turn - ((turn + MAGIC) - MAGIC)
+    frac = turn - jnp.round(turn)
     z = frac * frac
     hs = frac * horner(SIN_C, z)
     hc = horner(COS_C, z)
@@ -78,8 +78,8 @@
     return pos, pos, ad, da
 
 
-def pair_kernel(batches, groups, lists_ref, rows_ref, cen_ref, nor_ref, tan_ref, area_ref, fwd_ref, col_out, row_out, table, racc, ctab):
-    tiles = lists_ref.shape[0]
+def pair_kernel(batches, groups, lists_ref, rows_ref, cen_ref, nor_ref, tan_ref, area_ref, fwd_ref, col_out, row_out, table, racc, ctab, colv):
+    tiles = lists_ref.shape[0] // 256
     rt = jnp.transpose(rows_ref[...])
     for g in range(groups):
         for q in range(5):
@@ -104,48 +104,46 @@
 
     def tile_body(t, _):
         lanes = pl.ds(pl.multiple_of(t * 128, 128), 128)
-
-        def bc(i):
-            return jnp.broadcast_to(ctab[i:i + 1, lanes], (8, 128))
+        for i in range(15):
+            colv[i] = jnp.broadcast_to(ctab[i:i + 1, lanes], (8, 128))
+        for kind, weight in enumerate((1.0, 0.5, 1.0 / 3.0)):
+            for part in range(2):
+                colv[15 + 2 * kind + part] = jnp.broadcast_to(ctab[15 + part:16 + part, lanes] * weight, (8, 128))
 
         def getcol():
-            return dict(y=[bc(0), bc(1), bc(2)], n=[bc(3), bc(4), bc(5)], ts=[bc(6), bc(7), bc(8)],
-                        t2=[bc(9), bc(10), bc(11)], a=bc(12), at=bc(13), tn=bc(14))
+            return dict(y=[colv[0], colv[1], colv[2]], n=[colv[3], colv[4], colv[5]], ts=[colv[6], colv[7], colv[8]],
+                        t2=[colv[9], colv[10], colv[11]], a=colv[12], at=colv[13], tn=colv[14])
         zero = jnp.zeros((8, 128), F32)
-        n0, n1, n2 = lists_ref[t, 253], lists_ref[t, 254], lists_ref[t, 255]
-        b0, b1, b2 = batches
-        s0 = 0
-        s1 = n0 * b0
-        s2 = s1 + n1 * b1
-        carry = (zero,) * 7
-
-        def make(kind, size, start, weight):
-            def body(it, acc):
+
+        def make(kind, size):
+            def body(it, state):
+                pos, ids, acc = state
                 col = getcol()
-                frs, fis = bc(15) * weight, bc(16) * weight
+                frs, fis = colv[15 + 2 * kind], colv[16 + 2 * kind]
                 acc = list(acc)
-                ids, news = [], []
+                news = []
                 for j in range(size):
-                    g = lists_ref[t, start + it * size + j]
-                    row = [table[g, q] for q in range(5)]
-                    pos, cpos, ad, da = tile_terms(kind, row, col, frs, fis)
+                    row = [table[ids[j], q] for q in range(5)]
+                    gain, _, ad, da = tile_terms(kind, row, col, frs, fis)
                     for q in range(3):
-                        acc[q] = acc[q] + pos[q]
+                        acc[q] = acc[q] + gain[q]
                         acc[3 + q] = acc[3 + q] + ad[q]
                     if da is not None:
                         acc[6] = acc[6] + da
-                    ids.append(g)
-                    news.append(pos)
-                olds = [[racc[g, q] for q in range(3)] for g in ids]
-                for g, old, new in zip(ids, olds, news):
+                    news.append(gain)
+                olds = [[racc[ids[j], q] for q in range(3)] for j in range(size)]
+                for j in range(size):
                     for q in range(3):
-                        racc[g, q] = old[q] + new[q]
-                return tuple(acc)
+                        racc[ids[j], q] = olds[j][q] + news[j][q]
+                pos = pos + size
+                return pos, tuple(lists_ref[pos + j] for j in range(most)), tuple(acc)
             return body
-        carry = lax.fori_loop(0, n0, make(0, b0, s0, 1.0), carry)
-        carry = lax.fori_loop(0, n1, make(1, b1, s1, 0.5), carry)
-        carry = lax.fori_loop(0, n2, make(2, b2, s2, 1.0 / 3.0), carry)
-        sums = [jnp.sum(v, axis=0, keepdims=True) for v in carry]
+        most = max(batches)
+        start = t * 256
+        state = (start, tuple(lists_ref[start + j] for j in range(most)), (zero,) * 7)
+        for kind in range(3):
+            state = lax.fori_loop(0, lists_ref[start + 253 + kind], make(kind, batches[kind]), state)
+        sums = [jnp.sum(v, axis=0, keepdims=True) for v in state[2]]
         for q in range(3):
             col_out[q:q + 1, lanes] = -sums[q]
             tsr = ctab[6 + q:7 + q, lanes]
@@ -173,8 +171,8 @@
         in_specs=[pl.BlockSpec(memory_space=pltpu.SMEM)] + [vm] * 6,
         out_specs=(vm, vm),
         scratch_shapes=[pltpu.VMEM((groups + 1, 5, 8, 128), F32), pltpu.VMEM((groups + 1, 3, 8, 128), F32),
-                        pltpu.VMEM((24, el), F32)],
-        name="pairs",
+                        pltpu.VMEM((24, el), F32), pltpu.VMEM((21, 8, 128), F32)],
+        compiler_params=pltpu.CompilerParams(vmem_limit_bytes=16 << 20), name="pairs",
     )(lists, rows, cen, nor, tan, area, fwd)
 
 
@@ -378,7 +376,10 @@
     flag_swap.start()
     flag_swap.receive()
     flags = jnp.concatenate([flagall[r] for r in range(N_ROW)], axis=1).astype(F32)
-    lists_out[...] = make_lists(flags, BATCHES)
+    lists = make_lists(flags, BATCHES)
+    for t in range(8):
+        for half in range(2):
+            lists_out[2 * t + half:2 * t + half + 1, :] = lists[t:t + 1, half * 128:(half + 1) * 128]
     col_swap.receive()
     row_swap.start()
     rowall[pl.ds(pl.multiple_of(me["row"] * N_COL, N_COL), N_COL), :] = rowblk[...]
@@ -479,13 +480,13 @@
     flags = jnp.transpose(quad_order[:, :, 0, :], (1, 2, 0))
     rows, lists, codes = pl.pallas_call(
         gather_kernel,
-        out_shape=(S((128, 128), F32), S((8, 256), I32), S((3, el), I32)),
+        out_shape=(S((128, 128), F32), S((16, 128), I32), S((3, el), I32)),
         in_specs=[VM] * 5, out_specs=(VM,) * 3,
         scratch_shapes=[pltpu.VMEM((1, 128), F32), pltpu.VMEM((16, 128), F32), pltpu.VMEM((128, 128), F32),
                         pltpu.VMEM((8, 8, 16), I32)] + swap_sems(8) + swap_sems(16) + swap_sems(8),
-        compiler_params=pltpu.CompilerParams(collective_id=0, has_side_effects=True), name="gather",
+        compiler_params=pltpu.CompilerParams(collective_id=0, has_side_effects=True, vmem_limit_bytes=16 << 20), name="gather",
     )(centroid, adjoint_field, flags, slot_map.reshape(512, 128), corners)
-    col_part, row_part = pair_call(lists, rows, centroid, normals, tangent, element_area[None, :], forward_field, BATCHES)
+    col_part, row_part = pair_call(lists.reshape(2048), rows, centroid, normals, tangent, element_area[None, :], forward_field, BATCHES)
     vertex, grad = pl.pallas_call(
         finish_kernel,
         out_shape=(S((6, 512), F32), S((1, 384), F32)),
@@ -495,10 +496,10 @@
                         pltpu.VMEM((16, 8, 256), F32), pltpu.VMEM((16, 8, 256), F32), pltpu.VMEM((384, 128), F32),
                         pltpu.VMEM((1, 384), F32), pltpu.VMEM((8, 1, 384), F32), pltpu.VMEM((1, 384), F32),
                         pltpu.VMEM((16, 1, 384), F32), DMA] + (swap_sems(8) + swap_sems(16)) * 3,
-        compiler_params=pltpu.CompilerParams(collective_id=1, has_side_effects=True), name="finish",
+        compiler_params=pltpu.CompilerParams(collective_id=1, has_side_effects=True, vmem_limit_bytes=16 << 20), name="finish",
     )(col_part, row_part, codes, modes_t)
     return pl.pallas_call(emit_kernel, out_shape=(S((6, 512), F32), S((300,), F32)), in_specs=[VM] * 2, out_specs=(VM, VM),
-                          name="emit")(vertex, grad)
+                          compiler_params=pltpu.CompilerParams(vmem_limit_bytes=16 << 20), name="emit")(vertex, grad)
 
 
 def solution(mesh):

time: 77.8 us -> 81 us (1.041)
  local copies, waits for them, and re-layouts: 0 us -> 8.7 us
  Pallas kernels: 77.1 us -> 71 us
    unnamed x0 -> x20, local copies, waits for them, and re-layouts: none -> 8.7 us
    pallas_call x1, Pallas kernels: 28.6 us -> 26.7 us  [body(): pl.pallas_call(finish_kernel, out_shape=(S((6, 512), F32), S((1, 384), F3...]
    pallas_call x1, Pallas kernels: 28.2 us -> 26.4 us  [pair_call(): pl.pallas_call(functools.partial(pair_kernel, batches, groups), out_shape...]
    pallas_call x1, Pallas kernels: 18.9 us -> 17.3 us  [body(): pl.pallas_call(gather_kernel, out_shape=(S((128, 128), F32), S((16, 128),...]
where the time goes in v4:
time: 81 us; the launch traced here: 80.4 us
  Pallas kernels  71 us (88%)
  local copies, waits for them, and re-layouts  8.7 us (11%)
    pallas_call x1, Pallas kernels, body(): pl.pallas_call(finish_kernel, out_shape=(S((6, 512), F32), S((1, 384), F3...  26.7 us
    pallas_call x1, Pallas kernels, pair_call(): pl.pallas_call(functools.partial(pair_kernel, batches, groups), out_shape...  26.4 us
    pallas_call x1, Pallas kernels, body(): pl.pallas_call(gather_kernel, out_shape=(S((128, 128), F32), S((16, 128),...  17.3 us
    unnamed x20, local copies, waits for them, and re-layouts  8.7 us

profile of v4, /device:TPU:1, one launch (start us, length us, event | category | flops | bytes accessed | tf_op | source)
XLA Modules:
  0.0 80.4 jit_solution(18225444300658800511)
XLA Ops:
  0.6 0.0 copy-start.1
  0.6 0.9 %copy-done.1 = s32[65536]{0:T(1024)S(1)} copy-done((s32[65536]{0:T(1024)S(1)}, s32[65536]{0:T(1024)}, u32[]{:S(2)}) %copy-start.1) | copy-done | bytes 262168
  1.6 0.0 copy-start.2
  1.6 0.7 copy-done.2
  2.3 0.0 copy-start.3
  2.3 0.8 copy-done.3
  3.1 0.0 copy-start.6
  3.1 0.7 copy-done.6
  3.8 0.0 copy-start.8
  3.8 0.7 copy-done.8
  4.5 17.3 %gather.1 = (f32[128,128]{1,0:T(8,128)S(1)}, s32[16,128]{1,0:T(8,128)S(1)}, s32[3,1024]{1,0:T(4,128)S(1)}) custom-call(f32[3,1024]{1,0:T(4,128)S(1)} %copy-done.2, f32[2,1024]{1,0:T(2,128)S(1)} %copy-done.8, s32[8,8,16]{2,1,0:T(8,128)S(1)} %bitcast.9, s32[512,128]{1,0:T(8,128)S(1)} %bitcast.8, s32[3,1024]{1,0:T(4,128)S(1)} %copy-done.6), custom_call_target="tpu_custom_call" | custom-call | tf_op jit(solution)/shard_map/gather/pallas_call | solution.py:481
  21.8 0.0 copy-start.4
  21.8 0.7 copy-done.4
  22.5 0.0 copy-start.5
  22.5 0.7 copy-done.5
  23.2 0.0 copy-start.7
  23.2 0.7 copy-done.7
  23.9 0.0 copy-start.9
  23.9 0.7 copy-done.9
  24.6 26.4 %pairs.1 = (f32[6,1024]{1,0:T(8,128)S(1)}, f32[24,128]{1,0:T(8,128)S(1)}) custom-call(s32[2048]{0:T(1024)S(1)} %bitcast.10, f32[128,128]{1,0:T(8,128)S(1)} %get-tuple-element.10.rows_ref, f32[3,1024]{1,0:T(4,128)S(1)} %copy-done.2, f32[3,1024]{1,0:T(4,128)S(1)} %copy-done.4, f32[3,1024]{1,0:T(4,128)S(1)} %copy-done.5, f32[1,1024]{1,0:T(1,128)S(1)} %bitcast.11, ...), custom_call_target="tpu_custom_call" | custom-call | tf_op jit(solution)/shard_map/pairs/pallas_call | solution.py:168
  51.0 0.0 copy-start
  51.0 2.0 %copy-done = f32[300,6,512]{2,0,1:T(8,128)S(1)} copy-done((f32[300,6,512]{2,0,1:T(8,128)S(1)}, f32[300,6,512]{2,0,1:T(8,128)}, u32[]{:S(2)}) %copy-start) | copy-done | bytes 3686424
  53.1 26.7 %finish.1 = (f32[6,512]{1,0:T(8,128)S(1)}, f32[1,384]{1,0:T(1,128)S(1)}) custom-call(f32[6,1024]{1,0:T(8,128)S(1)} %get-tuple-element.11.col_ref, f32[24,128]{1,0:T(8,128)S(1)} %get-tuple-element.12.row_ref, s32[3,1024]{1,0:T(4,128)S(1)} %get-tuple-element.13.codes_ref, f32[6,300,512]{2,1,0:T(8,128)S(1)} %bitcast.7), custom_call_target="tpu_custom_call" | custom-call | tf_op jit(solution)/shard_map/finish/pallas_call | solution.py:490
  79.8 0.6 emit.1
Async XLA Ops:
  0.6 1.0 %copy-start.1 = (s32[65536]{0:T(1024)S(1)}, s32[65536]{0:T(1024)}, u32[]{:S(2)}) copy-start(s32[65536]{0:T(1024)} %param.17) | copy-start | bytes 786436
  1.6 0.7 copy-start.2
  2.3 0.8 copy-start.3
  3.1 0.7 copy-start.6
  3.8 0.7 copy-start.8
  21.8 0.7 copy-start.4
  22.5 0.7 copy-start.5
  23.2 0.7 copy-start.7
  23.9 0.7 copy-start.9
  51.0 2.1 %copy-start = (f32[300,6,512]{2,0,1:T(8,128)S(1)}, f32[300,6,512]{2,0,1:T(8,128)}, u32[]{:S(2)}) copy-start(f32[300,6,512]{2,0,1:T(8,128)} %param.19) | copy-start | bytes 11059204

commit v5 on v4

--- a/solution.py
+++ b/solution.py
@@ -78,7 +78,9 @@
     return pos, pos, ad, da
 
 
-def pair_kernel(batches, groups, lists_ref, rows_ref, cen_ref, nor_ref, tan_ref, area_ref, fwd_ref, col_out, row_out, table, racc, ctab, colv):
+def pair_kernel(batches, groups, lists_ref, rows_ref, cen_hbm, nor_hbm, tan_hbm, area_hbm, fwd_hbm, col_out, row_out,
+                table, racc, ctab, colv, cen_ref, nor_ref, tan_ref, area_ref, fwd_ref, insem):
+    copies = fetch_all((cen_hbm, nor_hbm, tan_hbm, area_hbm, fwd_hbm), (cen_ref, nor_ref, tan_ref, area_ref, fwd_ref), insem)
     tiles = lists_ref.shape[0] // 256
     rt = jnp.transpose(rows_ref[...])
     for g in range(groups):
@@ -87,6 +89,8 @@
             table[g, q] = v * 4.0 if q < 3 else v
     table[groups] = jnp.concatenate([jnp.full((3, 8, 128), 1.0, F32), jnp.zeros((2, 8, 128), F32)], axis=0)
     racc[...] = jnp.zeros(racc.shape, F32)
+    for copy in copies:
+        copy.wait()
     area = area_ref[...]
     spread = jnp.sqrt(area) * 2.4
     ysc = 4.0 * cen_ref[...]
@@ -168,10 +172,12 @@
     return pl.pallas_call(
         functools.partial(pair_kernel, batches, groups),
         out_shape=(jax.ShapeDtypeStruct((6, el), F32), jax.ShapeDtypeStruct((24, 128), F32)),
-        in_specs=[pl.BlockSpec(memory_space=pltpu.SMEM)] + [vm] * 6,
+        in_specs=[pl.BlockSpec(memory_space=pltpu.SMEM), vm] + [pl.BlockSpec(memory_space=pltpu.HBM)] * 5,
         out_specs=(vm, vm),
         scratch_shapes=[pltpu.VMEM((groups + 1, 5, 8, 128), F32), pltpu.VMEM((groups + 1, 3, 8, 128), F32),
-                        pltpu.VMEM((24, el), F32), pltpu.VMEM((21, 8, 128), F32)],
+                        pltpu.VMEM((24, el), F32), pltpu.VMEM((21, 8, 128), F32), pltpu.VMEM((3, el), F32),
+                        pltpu.VMEM((3, el), F32), pltpu.VMEM((3, el), F32), pltpu.VMEM((1, el), F32), pltpu.VMEM((2, el), F32),
+                        pltpu.SemaphoreType.DMA((5,))],
         compiler_params=pltpu.CompilerParams(vmem_limit_bytes=16 << 20), name="pairs",
     )(lists, rows, cen, nor, tan, area, fwd)
 
@@ -301,6 +307,7 @@
 
 
 VM = pl.BlockSpec(memory_space=pltpu.VMEM)
+HB = pl.BlockSpec(memory_space=pltpu.HBM)
 SLAB_DEV = 8
 BATCHES = (8, 4, 4)
 N_ROW, N_COL = 8, 16
@@ -351,12 +358,23 @@
     return [DMA((n,)), DMA((n,))]
 
 
-def gather_kernel(cen_ref, adj_ref, flags_ref, table_ref, corners_ref, rows_out, lists_out, codes_out,
-                  own, rowblk, rowall, flagall, fs, fr, cs, cr, rs, rr):
+def fetch_all(sources, targets, sems):
+    copies = [pltpu.make_async_copy(src, dst, sems.at[i]) for i, (src, dst) in enumerate(zip(sources, targets))]
+    for copy in copies:
+        copy.start()
+    return copies
+
+
+def gather_kernel(cen_hbm, adj_hbm, flags_hbm, table_hbm, corners_hbm, rows_out, lists_out, codes_out,
+                  cen_ref, adj_ref, flags_ref, table_ref, corners_ref, insem, own, rowblk, rowall, flagall, fs, fr, cs, cr, rs, rr):
     me = {"row": lax.axis_index("row"), "col": lax.axis_index("col")}
+    copies = fetch_all((cen_hbm, adj_hbm, flags_hbm, table_hbm, corners_hbm),
+                       (cen_ref, adj_ref, flags_ref, table_ref, corners_ref), insem)
     barrier = greet(me)
     lane = iota((1, 128), 1)
     packed = jnp.zeros((1, 128), F32)
+    copies[0].wait()
+    copies[1].wait()
     for q in range(5):
         line = cen_ref[q:q + 1, 0:128] if q < 3 else adj_ref[q - 3:q - 2, 0:128]
         if q:
@@ -364,7 +382,10 @@
         packed = jnp.where((lane >> 3) == q, line, packed)
     own[...] = packed
     rowblk[pl.ds(me["col"], 1), :] = packed
+    copies[2].wait()
     flagall[me["row"]] = flags_ref[me["row"]]
+    copies[3].wait()
+    copies[4].wait()
     slots = lookup_slots(table_ref[...], corners_ref[...])
     codes_out[...] = slots * 32 + patch_ranks(slots >> 9).astype(I32)
     pl.semaphore_wait(barrier, N_ROW + N_COL - 2)
@@ -478,19 +499,25 @@
     el = centroid.shape[1]
     modes_t = jnp.transpose(morph_modes, (1, 0, 2))
     flags = jnp.transpose(quad_order[:, :, 0, :], (1, 2, 0))
+    table = slot_map.reshape(512, 128)
+    area = element_area[None, :]
+    centroid, normals, tangent, area, forward_field, adjoint_field, corners, table, flags, modes_t = [
+        pltpu.with_memory_space_constraint(x, pltpu.HBM)
+        for x in (centroid, normals, tangent, area, forward_field, adjoint_field, corners, table, flags, modes_t)]
     rows, lists, codes = pl.pallas_call(
         gather_kernel,
         out_shape=(S((128, 128), F32), S((16, 128), I32), S((3, el), I32)),
-        in_specs=[VM] * 5, out_specs=(VM,) * 3,
-        scratch_shapes=[pltpu.VMEM((1, 128), F32), pltpu.VMEM((16, 128), F32), pltpu.VMEM((128, 128), F32),
+        in_specs=[HB] * 5, out_specs=(VM,) * 3,
+        scratch_shapes=[pltpu.VMEM((3, el), F32), pltpu.VMEM((2, el), F32), pltpu.VMEM((8, 8, 16), I32),
+                        pltpu.VMEM((512, 128), I32), pltpu.VMEM((3, el), I32), DMA((5,)), pltpu.VMEM((1, 128), F32), pltpu.VMEM((16, 128), F32), pltpu.VMEM((128, 128), F32),
                         pltpu.VMEM((8, 8, 16), I32)] + swap_sems(8) + swap_sems(16) + swap_sems(8),
         compiler_params=pltpu.CompilerParams(collective_id=0, has_side_effects=True, vmem_limit_bytes=16 << 20), name="gather",
-    )(centroid, adjoint_field, flags, slot_map.reshape(512, 128), corners)
-    col_part, row_part = pair_call(lists.reshape(2048), rows, centroid, normals, tangent, element_area[None, :], forward_field, BATCHES)
+    )(centroid, adjoint_field, flags, table, corners)
+    col_part, row_part = pair_call(lists.reshape(2048), rows, centroid, normals, tangent, area, forward_field, BATCHES)
     vertex, grad = pl.pallas_call(
         finish_kernel,
         out_shape=(S((6, 512), F32), S((1, 384), F32)),
-        in_specs=[VM] * 3 + [pl.BlockSpec(memory_space=pl.ANY)], out_specs=(VM, VM),
+        in_specs=[VM] * 3 + [HB], out_specs=(VM, VM),
         scratch_shapes=[pltpu.VMEM((6, 300, 512), F32), pltpu.VMEM((8, 24, 128), F32), pltpu.VMEM((24, 128), F32),
                         pltpu.VMEM((16, 24, 128), F32), pltpu.VMEM((2, 128, 128), F32), pltpu.VMEM((2, 128, 128), F32),
                         pltpu.VMEM((16, 8, 256), F32), pltpu.VMEM((16, 8, 256), F32), pltpu.VMEM((384, 128), F32),

time: 81 us -> 72.5 us (0.90)
  local copies, waits for them, and re-layouts: 8.7 us -> 0 us
    unnamed x20 -> x0, local copies, waits for them, and re-layouts: 8.7 us -> none
    pallas_call x1, Pallas kernels: 17.3 us -> 18.1 us  [body(): pl.pallas_call(gather_kernel, out_shape=(S((128, 128), F32), S((16, 128),...]
where the time goes in v5:
time: 72.5 us; the launch traced here: 72.4 us
  Pallas kernels  71.8 us (99%)
    pallas_call x1, Pallas kernels, body(): pl.pallas_call(finish_kernel, out_shape=(S((6, 512), F32), S((1, 384), F3...  26.7 us
    pallas_call x1, Pallas kernels, pair_call(): pl.pallas_call(functools.partial(pair_kernel, batches, groups), out_shape...  26.4 us
    pallas_call x1, Pallas kernels, body(): pl.pallas_call(gather_kernel, out_shape=(S((128, 128), F32), S((16, 128),...  18.1 us

profile of v5, /device:TPU:1, one launch (start us, length us, event | category | flops | bytes accessed | tf_op | source)
XLA Modules:
  0.0 72.4 jit_solution(10840456951983079393)
XLA Ops:
  0.6 18.1 %gather.1 = (f32[128,128]{1,0:T(8,128)S(1)}, s32[16,128]{1,0:T(8,128)S(1)}, s32[3,1024]{1,0:T(4,128)S(1)}) custom-call(f32[3,1024]{1,0:T(4,128)} %cen_hbm.3, f32[2,1024]{1,0:T(2,128)} %adj_hbm.1, s32[8,8,16]{2,1,0:T(8,128)} %bitcast.10, s32[512,128]{1,0:T(8,128)} %bitcast.9, s32[3,1024]{1,0:T(4,128)} %corners_hbm.1), custom_call_target="tpu_custom_call" | custom-call | tf_op jit(solution)/shard_map/gather/pallas_call | solution.py:507
  18.7 26.4 %pairs.1 = (f32[6,1024]{1,0:T(8,128)S(1)}, f32[24,128]{1,0:T(8,128)S(1)}) custom-call(s32[2048]{0:T(1024)S(1)} %bitcast.7, f32[128,128]{1,0:T(8,128)S(1)} %get-tuple-element.10.rows_ref, f32[3,1024]{1,0:T(4,128)} %cen_hbm.3, f32[3,1024]{1,0:T(4,128)} %nor_hbm.1, f32[3,1024]{1,0:T(4,128)} %tan_hbm.1, f32[1,1024]{1,0:T(1,128)} %bitcast.11, f32[2,1024]{1,0:T(2,128)} %fwd_hbm.1), custom_call_target="tpu_custom_call" | custom-call | tf_op jit(solution)/shard_map/pairs/pallas_call | solution.py:172
  45.1 26.7 %finish.1 = (f32[6,512]{1,0:T(8,128)S(1)}, f32[1,384]{1,0:T(1,128)S(1)}) custom-call(f32[6,1024]{1,0:T(8,128)S(1)} %get-tuple-element.11.col_ref, f32[24,128]{1,0:T(8,128)S(1)} %get-tuple-element.12.row_ref, s32[3,1024]{1,0:T(4,128)S(1)} %get-tuple-element.13.codes_ref, f32[6,300,512]{2,1,0:T(8,128)} %bitcast.8), custom_call_target="tpu_custom_call" | custom-call | tf_op jit(solution)/shard_map/finish/pallas_call | solution.py:517
  71.8 0.6 emit.1

commit v6 on v4

--- a/solution.py
+++ b/solution.py
@@ -78,29 +78,9 @@
     return pos, pos, ad, da
 
 
-def pair_kernel(batches, groups, lists_ref, rows_ref, cen_ref, nor_ref, tan_ref, area_ref, fwd_ref, col_out, row_out, table, racc, ctab, colv):
+def pair_kernel(batches, lists_ref, table, ctab, col_out, racc, colv):
     tiles = lists_ref.shape[0] // 256
-    rt = jnp.transpose(rows_ref[...])
-    for g in range(groups):
-        for q in range(5):
-            v = jnp.broadcast_to(rt[q * 8:(q + 1) * 8, g:g + 1], (8, 128))
-            table[g, q] = v * 4.0 if q < 3 else v
-    table[groups] = jnp.concatenate([jnp.full((3, 8, 128), 1.0, F32), jnp.zeros((2, 8, 128), F32)], axis=0)
     racc[...] = jnp.zeros(racc.shape, F32)
-    area = area_ref[...]
-    spread = jnp.sqrt(area) * 2.4
-    ysc = 4.0 * cen_ref[...]
-    n16 = 16.0 * nor_ref[...]
-    ts = spread * tan_ref[...]
-    a16 = 16.0 * area
-    at = a16 + jnp.sum(ts * ts, axis=0, keepdims=True)
-    tn = jnp.sum(ts * n16, axis=0, keepdims=True)
-    fw = fwd_ref[...] * (area * (1.0 / math.pi))
-    rows = [ysc, n16, ts, 2.0 * ts, a16, at, tn, fw]
-    pos = 0
-    for r in rows:
-        ctab[pos:pos + r.shape[0], :] = r
-        pos += r.shape[0]
 
     def tile_body(t, _):
         lanes = pl.ds(pl.multiple_of(t * 128, 128), 128)
@@ -151,29 +131,17 @@
         return 0
 
     lax.fori_loop(0, tiles, tile_body, 0)
-    lane = lax.broadcasted_iota(jnp.int32, (8, 128), 1)
-    outs = [jnp.zeros((8, 128), F32) for _ in range(3)]
-    for g in range(groups):
-        for q in range(3):
-            s = jnp.sum(racc[g, q], axis=1, keepdims=True)
-            outs[q] = jnp.where(lane == g, s, outs[q])
-    for q in range(3):
-        row_out[q * 8:(q + 1) * 8, :] = outs[q]
-
-
-def pair_call(lists, rows, cen, nor, tan, area, fwd, batches=(8, 4, 4)):
-    el = cen.shape[1]
-    groups = rows.shape[0]
+
+def pair_call(lists, table, ctab, batches):
+    el = ctab.shape[1]
     vm = pl.BlockSpec(memory_space=pltpu.VMEM)
     return pl.pallas_call(
-        functools.partial(pair_kernel, batches, groups),
-        out_shape=(jax.ShapeDtypeStruct((6, el), F32), jax.ShapeDtypeStruct((24, 128), F32)),
-        in_specs=[pl.BlockSpec(memory_space=pltpu.SMEM)] + [vm] * 6,
-        out_specs=(vm, vm),
-        scratch_shapes=[pltpu.VMEM((groups + 1, 5, 8, 128), F32), pltpu.VMEM((groups + 1, 3, 8, 128), F32),
-                        pltpu.VMEM((24, el), F32), pltpu.VMEM((21, 8, 128), F32)],
+        functools.partial(pair_kernel, batches),
+        out_shape=(jax.ShapeDtypeStruct((6, el), F32), jax.ShapeDtypeStruct((table.shape[0], 3, 8, 128), F32)),
+        in_specs=[pl.BlockSpec(memory_space=pltpu.SMEM), vm, vm], out_specs=(vm, vm),
+        scratch_shapes=[pltpu.VMEM((21, 8, 128), F32)],
         compiler_params=pltpu.CompilerParams(vmem_limit_bytes=16 << 20), name="pairs",
-    )(lists, rows, cen, nor, tan, area, fwd)
+    )(lists, table, ctab)
 
 
 def dot_nn(a, b):
@@ -301,6 +269,7 @@
 
 
 VM = pl.BlockSpec(memory_space=pltpu.VMEM)
+HB = pl.BlockSpec(memory_space=pltpu.HBM)
 SLAB_DEV = 8
 BATCHES = (8, 4, 4)
 N_ROW, N_COL = 8, 16
@@ -351,14 +320,36 @@
     return [DMA((n,)), DMA((n,))]
 
 
-def gather_kernel(cen_ref, adj_ref, flags_ref, table_ref, corners_ref, rows_out, lists_out, codes_out,
+def fetch_all(sources, targets, sems):
+    copies = [pltpu.make_async_copy(src, dst, sems.at[i]) for i, (src, dst) in enumerate(zip(sources, targets))]
+    for copy in copies:
+        copy.start()
+    return copies
+
+
+def column_rows(cen, nor, tan, area, fwd):
+    ts = jnp.sqrt(area) * 2.4 * tan
+    n16 = 16.0 * nor
+    a16 = 16.0 * area
+    at = a16 + jnp.sum(ts * ts, axis=0, keepdims=True)
+    tn = jnp.sum(ts * n16, axis=0, keepdims=True)
+    return [4.0 * cen, n16, ts, 2.0 * ts, a16, at, tn, fwd * (area * (1.0 / math.pi))]
+
+
+def gather_kernel(cen_hbm, adj_hbm, flags_hbm, table_hbm, corners_hbm, nor_hbm, tan_hbm, area_hbm, fwd_hbm,
+                  rowtab, lists_out, codes_out, ctab,
+                  cen_ref, adj_ref, flags_ref, table_ref, corners_ref, nor_ref, tan_ref, area_ref, fwd_ref, insem,
                   own, rowblk, rowall, flagall, fs, fr, cs, cr, rs, rr):
     me = {"row": lax.axis_index("row"), "col": lax.axis_index("col")}
+    copies = fetch_all((cen_hbm, adj_hbm, flags_hbm, table_hbm, corners_hbm, nor_hbm, tan_hbm, area_hbm, fwd_hbm),
+                       (cen_ref, adj_ref, flags_ref, table_ref, corners_ref, nor_ref, tan_ref, area_ref, fwd_ref), insem)
     barrier = greet(me)
     lane = iota((1, 128), 1)
     packed = jnp.zeros((1, 128), F32)
+    for copy in copies:
+        copy.wait()
     for q in range(5):
-        line = cen_ref[q:q + 1, 0:128] if q < 3 else adj_ref[q - 3:q - 2, 0:128]
+        line = cen_ref[q:q + 1, 0:128] * 4.0 if q < 3 else adj_ref[q - 3:q - 2, 0:128]
         if q:
             line = pltpu.roll(line, 8 * q, 1)
         packed = jnp.where((lane >> 3) == q, line, packed)
@@ -367,25 +358,44 @@
     flagall[me["row"]] = flags_ref[me["row"]]
     slots = lookup_slots(table_ref[...], corners_ref[...])
     codes_out[...] = slots * 32 + patch_ranks(slots >> 9).astype(I32)
+    at = 0
+    for line in column_rows(cen_ref[...], nor_ref[...], tan_ref[...], area_ref[...], fwd_ref[...]):
+        ctab[at:at + line.shape[0], :] = line
+        at += line.shape[0]
+    ctab[at:, :] = jnp.zeros((ctab.shape[0] - at, ctab.shape[1]), F32)
+    rowtab[128] = jnp.concatenate([jnp.full((3, 8, 128), 1.0, F32), jnp.zeros((2, 8, 128), F32)], axis=0)
     pl.semaphore_wait(barrier, N_ROW + N_COL - 2)
+
+    def rows_of(slot):
+        return pl.ds(pl.multiple_of(slot * N_COL, N_COL), N_COL)
+
     flag_swap = Swap(me, "row", N_ROW, lambda peer: flags_ref.at[peer], lambda slot: flagall.at[slot], (fs, fr))
     col_swap = Swap(me, "col", N_COL, lambda peer: own, lambda slot: rowblk.at[pl.ds(slot, 1), :], (cs, cr))
-    row_swap = Swap(me, "row", N_ROW, lambda peer: rowblk,
-                    lambda slot: rowall.at[pl.ds(pl.multiple_of(slot * N_COL, N_COL), N_COL), :], (rs, rr))
+    row_swap = Swap(me, "row", N_ROW, lambda peer: rowblk, lambda slot: rowall.at[rows_of(slot), :], (rs, rr))
+
+    def spread(block, slot):
+        turned = jnp.transpose(block)[0:40]
+        for c in range(N_COL):
+            for q in range(5):
+                rowtab[c * N_ROW + slot, q] = jnp.broadcast_to(turned[q * 8:(q + 1) * 8, c:c + 1], (8, 128))
+
     col_swap.start()
     flag_swap.start()
+    col_swap.receive()
+    row_swap.start()
+    spread(rowblk[...], me["row"])
     flag_swap.receive()
     flags = jnp.concatenate([flagall[r] for r in range(N_ROW)], axis=1).astype(F32)
     lists = make_lists(flags, BATCHES)
     for t in range(8):
         for half in range(2):
             lists_out[2 * t + half:2 * t + half + 1, :] = lists[t:t + 1, half * 128:(half + 1) * 128]
-    col_swap.receive()
-    row_swap.start()
-    rowall[pl.ds(pl.multiple_of(me["row"] * N_COL, N_COL), N_COL), :] = rowblk[...]
-    row_swap.receive()
-    for c in range(N_COL):
-        rows_out[c * N_ROW:(c + 1) * N_ROW, :] = rowall[pl.ds(c, N_ROW, stride=N_COL), :]
+    chip, core = me["row"] // 2, lax.rem(me["row"], 2)
+    for away in (0, 1, 3, 2):
+        for other in ((1,) if away == 0 else (0, 1)):
+            peer = lax.rem(chip + away, N_ROW // 2) * 2 + lax.rem(core + other, 2)
+            row_swap.copy(peer, peer).wait_recv()
+            spread(rowall[rows_of(peer), :], peer)
     for swap in (col_swap, flag_swap, row_swap):
         swap.drain()
 
@@ -403,8 +413,8 @@
     return sum(dot_nt(ones, p) for p in split3(acc_ref[...]))
 
 
-def finish_kernel(col_ref, row_ref, codes_ref, modes_hbm, vertex_out, grad_out,
-                  modes, part8, sumrow, part16, send, mid, stage, recv, acc, grad, grad8, mid_grad, grad16,
+def finish_kernel(col_ref, racc_ref, codes_ref, modes_hbm, vertex_out, grad_out,
+                  modes, row_ref, part8, sumrow, part16, send, mid, stage, recv, acc, grad, grad8, mid_grad, grad16,
                   msem, a0, a1, b0, b1, c0, c1, d0, d1, e0, e1, f0, f1):
     me = {"row": lax.axis_index("row"), "col": lax.axis_index("col")}
     r, c = me["row"], me["col"]
@@ -433,6 +443,13 @@
             element = jnp.minimum(iota((1, width), 1) + cb * width, SLAB_DEV).astype(F32)
             eight = jnp.concatenate([col_ref[:, cols] * third, (slots & 511).astype(F32), element], axis=0)
             total = total + bucket_terms(eight, slots, code & 31)
+    lane = iota((8, 128), 1)
+    outs = [jnp.zeros((8, 128), F32) for _ in range(3)]
+    for g in range(128):
+        for q in range(3):
+            outs[q] = jnp.where(lane == g, jnp.sum(racc_ref[g, q], axis=1, keepdims=True), outs[q])
+    for q in range(3):
+        row_ref[q * 8:(q + 1) * 8, :] = outs[q]
     send[0] = total[:, 0:128]
     send[1] = jnp.concatenate([total[:, 128:192], jnp.zeros((128, 64), F32)], axis=1)
     pl.semaphore_wait(barrier, N_ROW + N_COL - 2)
@@ -478,20 +495,28 @@
     el = centroid.shape[1]
     modes_t = jnp.transpose(morph_modes, (1, 0, 2))
     flags = jnp.transpose(quad_order[:, :, 0, :], (1, 2, 0))
-    rows, lists, codes = pl.pallas_call(
+    table = slot_map.reshape(512, 128)
+    area = element_area[None, :]
+    centroid, normals, tangent, area, forward_field, adjoint_field, corners, table, flags, modes_t = [
+        pltpu.with_memory_space_constraint(x, pltpu.HBM)
+        for x in (centroid, normals, tangent, area, forward_field, adjoint_field, corners, table, flags, modes_t)]
+    rowtab, lists, codes, ctab = pl.pallas_call(
         gather_kernel,
-        out_shape=(S((128, 128), F32), S((16, 128), I32), S((3, el), I32)),
-        in_specs=[VM] * 5, out_specs=(VM,) * 3,
-        scratch_shapes=[pltpu.VMEM((1, 128), F32), pltpu.VMEM((16, 128), F32), pltpu.VMEM((128, 128), F32),
+        out_shape=(S((129, 5, 8, 128), F32), S((16, 128), I32), S((3, el), I32), S((24, el), F32)),
+        in_specs=[HB] * 9, out_specs=(VM,) * 4,
+        scratch_shapes=[pltpu.VMEM((3, el), F32), pltpu.VMEM((2, el), F32), pltpu.VMEM((8, 8, 16), I32),
+                        pltpu.VMEM((512, 128), I32), pltpu.VMEM((3, el), I32), pltpu.VMEM((3, el), F32), pltpu.VMEM((3, el), F32),
+                        pltpu.VMEM((1, el), F32), pltpu.VMEM((2, el), F32), DMA((9,)), pltpu.VMEM((1, 128), F32),
+                        pltpu.VMEM((16, 128), F32), pltpu.VMEM((128, 128), F32),
                         pltpu.VMEM((8, 8, 16), I32)] + swap_sems(8) + swap_sems(16) + swap_sems(8),
         compiler_params=pltpu.CompilerParams(collective_id=0, has_side_effects=True, vmem_limit_bytes=16 << 20), name="gather",
-    )(centroid, adjoint_field, flags, slot_map.reshape(512, 128), corners)
-    col_part, row_part = pair_call(lists.reshape(2048), rows, centroid, normals, tangent, element_area[None, :], forward_field, BATCHES)
+    )(centroid, adjoint_field, flags, table, corners, normals, tangent, area, forward_field)
+    col_part, row_part = pair_call(lists.reshape(2048), rowtab, ctab, BATCHES)
     vertex, grad = pl.pallas_call(
         finish_kernel,
         out_shape=(S((6, 512), F32), S((1, 384), F32)),
-        in_specs=[VM] * 3 + [pl.BlockSpec(memory_space=pl.ANY)], out_specs=(VM, VM),
-        scratch_shapes=[pltpu.VMEM((6, 300, 512), F32), pltpu.VMEM((8, 24, 128), F32), pltpu.VMEM((24, 128), F32),
+        in_specs=[VM] * 3 + [HB], out_specs=(VM, VM),
+        scratch_shapes=[pltpu.VMEM((6, 300, 512), F32), pltpu.VMEM((24, 128), F32), pltpu.VMEM((8, 24, 128), F32), pltpu.VMEM((24, 128), F32),
                         pltpu.VMEM((16, 24, 128), F32), pltpu.VMEM((2, 128, 128), F32), pltpu.VMEM((2, 128, 128), F32),
                         pltpu.VMEM((16, 8, 256), F32), pltpu.VMEM((16, 8, 256), F32), pltpu.VMEM((384, 128), F32),
                         pltpu.VMEM((1, 384), F32), pltpu.VMEM((8, 1, 384), F32), pltpu.VMEM((1, 384), F32),

time: 81 us -> 71.7 us (0.89)
  local copies, waits for them, and re-layouts: 8.7 us -> 0 us
    unnamed x20 -> x0, local copies, waits for them, and re-layouts: 8.7 us -> none
where the time goes in v6:
time: 71.7 us; the launch traced here: 71.6 us
  Pallas kernels  71 us (99%)
    pallas_call x1, Pallas kernels, body(): pl.pallas_call(finish_kernel, out_shape=(S((6, 512), F32), S((1, 384), F3...  27 us
    pallas_call x1, Pallas kernels, pair_call(): pl.pallas_call(functools.partial(pair_kernel, batches), out_shape=(jax.Sh...  24.7 us
    pallas_call x1, Pallas kernels, body(): pl.pallas_call(gather_kernel, out_shape=(S((129, 5, 8, 128), F32), S((16,...  18.7 us

profile of v6, /device:TPU:1, one launch (start us, length us, event | category | flops | bytes accessed | tf_op | source)
XLA Modules:
  0.0 71.6 jit_solution(6755398910078842565)
XLA Ops:
  0.6 18.7 %gather.1 = (f32[129,5,8,128]{3,2,1,0:T(8,128)S(1)}, s32[16,128]{1,0:T(8,128)S(1)}, s32[3,1024]{1,0:T(4,128)S(1)}, f32[24,1024]{1,0:T(8,128)S(1)}) custom-call(f32[3,1024]{1,0:T(4,128)} %cen_hbm.1, f32[2,1024]{1,0:T(2,128)} %adj_hbm.1, s32[8,8,16]{2,1,0:T(8,128)} %bitcast.10, s32[512,128]{1,0:T(8,128)} %bitcast.9, s32[3,1024]{1,0:T(4,128)} %corners_hbm.1, ...), custom_call_target="tpu_custom_call" | custom-call | tf_op jit(solution)/shard_map/gather/pallas_call | solution.py:503
  19.3 24.7 %pairs.1 = (f32[6,1024]{1,0:T(8,128)S(1)}, f32[129,3,8,128]{3,2,1,0:T(8,128)S(1)}) custom-call(s32[2048]{0:T(1024)S(1)} %bitcast.7, f32[129,5,8,128]{3,2,1,0:T(8,128)S(1)} %get-tuple-element.11.table, f32[24,1024]{1,0:T(8,128)S(1)} %get-tuple-element.12.ctab), custom_call_target="tpu_custom_call" | custom-call | tf_op jit(solution)/shard_map/pairs/pallas_call | solution.py:138
  44.0 27.0 %finish.1 = (f32[6,512]{1,0:T(8,128)S(1)}, f32[1,384]{1,0:T(1,128)S(1)}) custom-call(f32[6,1024]{1,0:T(8,128)S(1)} %get-tuple-element.13.col_ref, f32[129,3,8,128]{3,2,1,0:T(8,128)S(1)} %get-tuple-element.14.racc_ref, s32[3,1024]{1,0:T(4,128)S(1)} %get-tuple-element.15.codes_ref, f32[6,300,512]{2,1,0:T(8,128)} %bitcast.8), custom_call_target="tpu_custom_call" | custom-call | tf_op jit(solution)/shard_map/finish/pallas_call | solution.py:515
  71.0 0.6 emit.1
